TPU v7x, 256 devices: a whole 4x4x8 slice. The times are simulated.
256 devices in a mesh: docs: 64 (over x, z, core), terms: 4 (over y).
Axes of the slice: x: 4, y: 4, z: 8, core: 2. Of those that a mesh axis runs over, the one named last changes fastest.
Arguments:
- values: bfloat16 [256, 64, 64, 128], P('docs', 'terms')
- block_ids: int32 [256, 64], P('docs', 'terms'), may hold values from 0 to 2047, as said below
- assignment: int32 [16384, 1], P('docs'), may hold values from 0 to 511
Outputs:
- coefficients: float32 [16384, 512], P('docs', 'terms')
Inputs may be any that keep to these rules, and one draw needn't show every extreme that they name: `assignment`: every one of the 512 clusters has at least one document. `block_ids`: in each term slice, the 16 blocks of one tile lie in 16 different ranges of 32 consecutive block numbers, and the tiles of one index of docs place exactly 1 block in each such range.
All inputs are finite; a program needn't handle non-finite values.
Results may differ from a plain program's by a relative error of at most 0.00045.
Values may be sent and summed in bfloat16 or wider, within the bound.
A program may use at most 128 MiB of HBM per device.

v0:
```python
import jax
import jax.numpy as jnp
from jax import lax
from jax.sharding import PartitionSpec as P

K = 512
BLK_OWN = 32


EPSILON = 1e-06
RIDGE_WEIGHT = 1.0


def send_order(owner, capacity):
    pairs = owner.shape[0]
    counter = jnp.arange(pairs, dtype=jnp.int32)
    same = owner[:, None] == owner[None, :]
    earlier = counter[None, :] < counter[:, None]
    rank = jnp.sum((same & earlier).astype(jnp.int32), axis=1)
    target = owner * capacity + rank
    source = jnp.zeros((pairs,), jnp.int32).at[target].set(counter)
    return (target, source)


def pick_tile(labels, tile_index):
    return labels[tile_index]


def body(values, block_ids, assignment):
    tiles_here, slot_count, tile_rows, block_width = values.shape
    peers = lax.axis_size("docs")
    pairs = tiles_here * slot_count
    capacity = pairs // peers
    arrivals = peers * capacity
    doc_rows = tiles_here * tile_rows
    all_blocks, all_labels = (
        lax.all_gather(block_ids, "docs", axis=0, tiled=True),
        lax.all_gather(assignment, "docs", axis=0, tiled=True),
    )
    own_target, own_source = send_order((block_ids // BLK_OWN).reshape(pairs), capacity)
    flat_values = values.reshape(pairs, tile_rows, block_width)
    outgoing = flat_values[own_source].reshape(peers, capacity, tile_rows, block_width)
    arrived = lax.all_to_all(outgoing, "docs", split_axis=0, concat_axis=0, tiled=True)
    arrived = arrived.reshape(arrivals, tile_rows, block_width)
    sender_blocks = all_blocks.reshape(peers, pairs)

    def sender_source(blocks):
        return send_order(blocks // BLK_OWN, capacity)[1]

    sender_sources = jax.vmap(sender_source)(sender_blocks)
    mine = lax.dynamic_slice_in_dim(sender_sources, lax.axis_index("docs") * capacity, capacity, 1)
    local_block = (jnp.take_along_axis(sender_blocks, mine, axis=1) % BLK_OWN).reshape(arrivals)
    tile_of = mine // slot_count
    sender_labels = all_labels[:, 0].reshape(peers, tiles_here, tile_rows)
    arrived_labels = jax.vmap(pick_tile)(sender_labels, tile_of).reshape(arrivals, tile_rows)
    cluster_hot = (
        arrived_labels[:, :, None] == jnp.arange(K, dtype=jnp.int32)[None, None, :]
    ).astype(jnp.bfloat16)
    contrib = jnp.einsum("rtk,rtb->rkb", cluster_hot, arrived, preferred_element_type=jnp.float32)
    block_hot = (local_block[:, None] == jnp.arange(BLK_OWN, dtype=jnp.int32)[None, :]).astype(
        jnp.float32
    )
    sums_own = jnp.einsum(
        "rc,rkb->kcb",
        block_hot,
        contrib,
        precision=lax.Precision.HIGHEST,
        preferred_element_type=jnp.float32,
    )
    sums_own = sums_own.reshape(K, BLK_OWN * block_width)
    sq_total = lax.psum(jnp.sum(sums_own * sums_own, axis=1), ("docs", "terms"))
    concepts_own = (sums_own * lax.rsqrt(sq_total + EPSILON)[:, None]).astype(jnp.bfloat16)
    gram_part = jnp.dot(concepts_own, concepts_own.T, preferred_element_type=jnp.float32)
    gram_matrix = lax.psum(gram_part, ("docs", "terms"))
    identity = jnp.eye(K, dtype=jnp.float32)
    factor = jnp.linalg.cholesky(gram_matrix + RIDGE_WEIGHT * identity)
    inverse = jax.scipy.linalg.cho_solve((factor, True), identity)
    concept_blocks = jnp.transpose(concepts_own.reshape(K, BLK_OWN, block_width), (1, 0, 2))
    wanted = concept_blocks[local_block]
    reply = lax.all_to_all(
        wanted.reshape(peers, capacity, K, block_width),
        "docs",
        split_axis=0,
        concat_axis=0,
        tiled=True,
    )
    fetched = reply.reshape(pairs, K, block_width)[own_target].reshape(
        tiles_here, slot_count, K, block_width
    )
    scores_part = jnp.einsum("isrb,iskb->irk", values, fetched, preferred_element_type=jnp.float32)
    scores_part = scores_part.reshape(doc_rows, K)
    col_width = K // lax.axis_size("terms")
    scores = lax.psum(scores_part, "terms")
    inverse_cols = lax.dynamic_slice_in_dim(
        inverse, lax.axis_index("terms") * col_width, col_width, 1
    )
    return jnp.dot(
        scores, inverse_cols, precision=lax.Precision.HIGHEST, preferred_element_type=jnp.float32
    )


def solution(mesh):
    in_specs = (P("docs", "terms", None, None), P("docs", "terms"), P("docs", None))
    out_specs = P("docs", "terms")
    return jax.shard_map(body, mesh=mesh, in_specs=in_specs, out_specs=out_specs, check_vma=False)
```

profile of v0, /device:TPU:2, one launch (start us, length us, event | category | flops | bytes accessed | tf_op | source)
XLA Modules:
  0.0 813.5 jit_solution(112224903261461516)
XLA Ops:
  7.4 0.8 add_select_fusion.5
  8.7 0.8 scatter_custom_fusion
  9.5 1.7 gather_fusion
  11.2 12.0 %all-to-all-start = ((bf16[64,1,64,128]{3,2,1,0:T(8,128)(2,1)}), bf16[64,1,64,128]{3,2,1,0:T(8,128)(2,1)S(1)}, u32[]{:S(2)}, u32[]{:S(2)}) async-start(bf16[64,1,64,128]{3,2,1,0:T(8,128)(2,1)} %bitcast.7), calls=%async_computation | async-start | bytes 2097152 | tf_op jit(solution)/shard_map/all_to_all | solution.py:43
  23.3 67.7 %all-gather = s32[64,4,16]{2,1,0:T(4,128)S(1)} all-gather(s32[1,4,16]{2,1,0:T(4,128)} %bitcast.108), channel_id=1, replica_groups=mesh['docs'=64,'terms'=4] {'docs'}, dimensions={0}, use_global_device_ids=true | all-gather | bytes 16640 | tf_op jit(solution)/shard_map/all_gather | solution.py:37
  91.2 1.9 convert_reduce_fusion
  93.2 0.7 multiply_reduce_fusion.1
  94.1 15.5 %scatter_custom_fusion.1 = s32[4096]{0:T(1024)S(1)} fusion(s32[4096]{0:T(1024)S(1)} %reshape.365, s32[4096]{0:T(1024)S(1)} %reshape.367, s32[]{:T(128)} %copy.156), kind=kCustom, calls=%fused_computation.147 | custom fusion | bytes 16388
  110.1 41.3 %all_gather.6 = s32[16384,1]{0,1:T(1,128)S(1)} all-gather(s32[256,1]{0,1:T(1,128)} %param.5), channel_id=1, replica_groups=mesh['docs'=64,'terms'=4] {'docs'}, dimensions={0}, use_global_device_ids=true | all-gather | bytes 66560 | tf_op jit(solution)/shard_map/all_gather | solution.py:38
  151.4 0.6 broadcast.507
  152.0 0.9 reduce.46
  153.2 0.8 gather_fusion.4
  154.3 0.8 gather_fusion.3
  155.3 5.5 fusion.2
  160.8 26.4 %multiply_reduce_fusion = (f32[512]{0:T(512)S(1)}, f32[512,128,32]{1,2,0:T(8,128)}) fusion(s32[64]{0:T(128)S(1)} %get-tuple-element.14, f32[64,512,128]{2,1,0:T(8,128)S(1)} %fusion.2), kind=kOutput, calls=%fused_computation.12 | convolution fusion | flops 1614808576 | bytes 25168128 | tf_op jit(solution)/shard_map/rc,rkb->kcb/dot_general | solution.py:63
  187.2 77.1 %psum.21 = f32[512]{0:T(512)S(1)} all-reduce(f32[512]{0:T(512)S(1)} %get-tuple-element.45), channel_id=1, replica_groups=mesh['docs'=64,'terms'=4] {'docs','terms'}, use_global_device_ids=true, to_apply=%region_5.6 | all-reduce | flops 512 | bytes 4096 | tf_op jit(solution)/shard_map/psum | solution.py:71
  264.3 5.6 fusion.88
  269.9 3.5 copy.113
  273.4 7.7 gather_fusion.1
  281.1 9.2 %all-to-all-start.1 = ((bf16[64,1,512,128]{3,2,1,0:T(8,128)(2,1)}), bf16[64,1,512,128]{3,2,1,0:T(8,128)(2,1)}, u32[]{:S(2)}, u32[]{:S(2)}) async-start(bf16[64,1,512,128]{3,2,1,0:T(8,128)(2,1)} %bitcast.103), calls=%async_computation.1 | async-start | bytes 16777216 | tf_op jit(solution)/shard_map/all_to_all | solution.py:80
  290.4 6.9 fusion.6
  297.6 0.8 iota_compare_fusion.2
  298.4 1.1 fusion.27
  299.5 293.0 %all-reduce.6.cloned.1.call-done = f32[512,512]{0,1:T(8,128)} async-done(((f32[512,512]{0,1:T(8,128)}), f32[512,512]{0,1:T(8,128)}) %all-reduce.6.cloned.1.call-update) | async-done | bytes 1048592 | tf_op jit(solution)/shard_map/psum | solution.py:74
  592.5 1.3 convert_add_fusion
  594.2 1.4 fusion.9
  595.7 11.7 %cholesky.104 = f32[128,128]{1,0:T(8,128)S(1)} custom-call(f32[128,128]{1,0:T(8,128)S(1)} %cholesky.266), custom_call_target="Cholesky" | custom-call | tf_op jit(solution)/shard_map/jit(cholesky)/cholesky | solution.py:76
  607.5 9.8 %custom-call.34 = f32[1,128,128]{1,2,0:T(8,128)S(1)} custom-call(f32[1,128,128]{2,1,0:T(8,128)S(1)} %get-tuple-element.38), custom_call_target="InvertDiagBlocksLowerTriangular" | custom-call | tf_op jit(solution)/shard_map/jit(cholesky)/cholesky | solution.py:76
  618.0 11.7 %cholesky.217 = f32[128,128]{1,0:T(8,128)S(1)} custom-call(f32[128,128]{1,0:T(8,128)S(1)} %cholesky.270), custom_call_target="Cholesky" | custom-call | tf_op jit(solution)/shard_map/jit(cholesky)/cholesky | solution.py:76
  629.8 10.0 %custom-call.35 = f32[1,128,128]{1,2,0:T(8,128)S(1)} custom-call(f32[1,128,128]{2,1,0:T(8,128)S(1)} %get-tuple-element.35), custom_call_target="InvertDiagBlocksLowerTriangular" | custom-call | tf_op jit(solution)/shard_map/jit(cholesky)/cholesky | solution.py:76
  640.0 0.4 convolution_subtract_fusion.7
  640.4 11.7 %cholesky.238 = f32[128,128]{1,0:T(8,128)S(1)} custom-call(f32[128,128]{1,0:T(8,128)S(1)} %cholesky.275), custom_call_target="Cholesky" | custom-call | tf_op jit(solution)/shard_map/jit(cholesky)/cholesky | solution.py:76
  652.2 9.8 %custom-call.36 = f32[1,128,128]{1,2,0:T(8,128)S(1)} custom-call(f32[1,128,128]{2,1,0:T(8,128)S(1)} %get-tuple-element.32), custom_call_target="InvertDiagBlocksLowerTriangular" | custom-call | tf_op jit(solution)/shard_map/jit(cholesky)/cholesky | solution.py:76
  662.2 0.4 convolution_subtract_fusion.8
  662.6 11.7 %cholesky.255 = f32[128,128]{1,0:T(8,128)S(1)} custom-call(f32[128,128]{1,0:T(8,128)S(1)} %convolution_subtract_fusion.8), custom_call_target="Cholesky" | custom-call | tf_op jit(solution)/shard_map/jit(cholesky)/cholesky | solution.py:76
  674.3 1.1 compare_reduce_fusion.2
  675.4 0.6 compare_reduce_fusion.3
  677.3 0.6 compare_reduce_fusion.1
  678.6 0.6 compare_reduce_fusion
  679.9 10.5 %while.1 = (s32[]{:T(128)}, f32[512,512]{1,0:T(8,128)S(1)}, s32[4,2]{0,1:T(2,128)S(1)}, f32[4,128,128]{2,1,0:T(8,128)}, s32[]{:T(128)}) while((s32[]{:T(128)}, f32[512,512]{1,0:T(8,128)S(1)}, s32[4,2]{0,1:T(2,128)S(1)}, f32[4,128,128]{2,1,0:T(8,128)}, s32[]{:T(128)}) %tuple.35), condition=%wide.while_cond, body=%wide.while_body.sunk | while | flops 2 | bytes 132705 | solution.py:77
  680.0 0.6 fusion.108
  680.6 2.0 bitcast_dynamic-update-slice_fusion.2
  682.6 0.6 fusion.108
  683.2 2.0 bitcast_dynamic-update-slice_fusion.2
  685.2 0.6 fusion.108
  685.8 2.0 bitcast_dynamic-update-slice_fusion.2
  687.9 0.6 fusion.108
  688.5 2.0 bitcast_dynamic-update-slice_fusion.2
  690.4 40.1 %custom-call.37 = f32[4,128,128]{1,2,0:T(8,128)S(1)} custom-call(f32[4,128,128]{2,1,0:T(8,128)} %get-tuple-element.12), custom_call_target="InvertDiagBlocksLowerTriangular" | custom-call | tf_op jit(solution)/shard_map/jit(_cho_solve)/triangular_solve | solution.py:77
  730.5 1.1 fusion.34
  731.6 1.5 convolution_subtract_fusion.3
  733.2 0.4 fusion.54
  733.6 1.9 convolution_subtract_fusion.2
  735.6 0.4 fusion.56
  736.0 2.4 convolution_subtract_fusion.5
  738.4 0.4 fusion.58
  739.2 0.4 convolution_subtract_fusion.1
  740.0 1.2 convolution_subtract_fusion
  741.2 8.9 %gather_fusion.2 = bf16[64,512,128]{2,1,0:T(8,128)(2,1)} fusion(bf16[64,512,128]{2,1,0:T(8,128)(2,1)} %bitcast.15, s32[1024]{0:T(1024)S(1)} %pad_clamp_fusion), kind=kCustom, calls=%fused_computation.2 | custom fusion | bytes 16777472 | tf_op jit(solution)/shard_map/gather | solution.py:87
  750.1 6.8 fusion.93
  756.9 1.3 fusion.53
  758.2 0.7 convolution_subtract_fusion.4
  759.3 44.3 %all-reduce.4.cloned.1.call-done = f32[256,512]{1,0:T(8,128)} async-done(((f32[256,512]{1,0:T(8,128)}), f32[256,512]{1,0:T(8,128)}) %all-reduce.4.cloned.1.call-update) | async-done | bytes 524304 | tf_op jit(solution)/shard_map/psum | solution.py:93
  803.6 2.3 fusion.31
  (69 shorter events, 5.9 us)
Async XLA Ops:
  7.4 2.2 copy-start
  11.2 144.1 %all-to-all-start = ((bf16[64,1,64,128]{3,2,1,0:T(8,128)(2,1)}), bf16[64,1,64,128]{3,2,1,0:T(8,128)(2,1)S(1)}, u32[]{:S(2)}, u32[]{:S(2)}) async-start(bf16[64,1,64,128]{3,2,1,0:T(8,128)(2,1)} %bitcast.7), calls=%async_computation | async-start | bytes 2097152 | tf_op jit(solution)/shard_map/all_to_all | solution.py:43
  281.1 460.0 %all-to-all-start.1 = ((bf16[64,1,512,128]{3,2,1,0:T(8,128)(2,1)}), bf16[64,1,512,128]{3,2,1,0:T(8,128)(2,1)}, u32[]{:S(2)}, u32[]{:S(2)}) async-start(bf16[64,1,512,128]{3,2,1,0:T(8,128)(2,1)} %bitcast.103), calls=%async_computation.1 | async-start | bytes 16777216 | tf_op jit(solution)/shard_map/all_to_all | solution.py:80
  290.4 302.2 %all-reduce.6.cloned.1.call-start = ((), (), s32[]{:S(2)}) async-start(), calls=%async_computation.3 | async-start | bytes 2097152 | tf_op jit(solution)/shard_map/psum | solution.py:74
  297.3 506.3 %all-reduce.4.cloned.1.call-start = ((), (), s32[]{:S(2)}) async-start(), calls=%async_computation.2 | async-start | bytes 1048576 | tf_op jit(solution)/shard_map/psum | solution.py:93
Sparse Core Ops, SparseCore 0:
  297.4 295.0 all-reduce.5
Sparse Core Ops, SparseCore 1:
  757.0 46.6 all-reduce.3
where the time goes:
time: 821 us; the launch traced here: 813 us
  waiting for transfers between devices  337 us (41%)
  blocking collectives  186 us (23%)
  other arithmetic  135 us (16%)
  matrix products  62.6 us (8%)
  local copies, waits for them, and re-layouts  52.6 us (6%)
  starting transfers between devices  21.5 us (3%)
  between operations  17.9 us (2%)
    psum x1, waiting for transfers between devices, body(): gram_matrix = lax.psum(gram_part, ('docs', 'terms'))  293 us
    another operation x15, other arithmetic, body(): factor = jnp.linalg.cholesky(gram_matrix + RIDGE_WEIGHT * identity)  79.6 us
    psum x1, blocking collectives, body(): sq_total = lax.psum(jnp.sum(sums_own * sums_own, axis=1), ('docs', 'terms'))  77.1 us
    all_gather x1, blocking collectives, body(): lax.all_gather(block_ids, 'docs', axis=0, tiled=True)  67.7 us
    psum x1, waiting for transfers between devices, body(): scores = lax.psum(scores_part, 'terms')  44.3 us
    all_gather x1, blocking collectives, body(): lax.all_gather(assignment, 'docs', axis=0, tiled=True)  41.3 us
    another operation x3, other arithmetic, body(): inverse = jax.scipy.linalg.cho_solve((factor, True), identity)  40.3 us
    dot_general x1, matrix products, body(): jnp.einsum('rc,rkb->kcb', block_hot, contrib, precision=lax.Precision.HIG...  26.4 us
  transfers between devices with their start and end apart: 4, of which 2 were waited for; matrix products, arithmetic and copies ran while one was open for 22% of the time, Pallas kernels for 0%

commit v1 on v0

v1 whole, which is shorter than its diff:
```python
import functools

import jax
import jax.numpy as jnp
from jax import lax
from jax.experimental import pallas as pl
from jax.experimental.pallas import tpu as pltpu
from jax.sharding import PartitionSpec as P

K = 512
BLK_OWN = 32
NX = 4
NZ = 8
NC = 2
EPSILON = 1e-06
RIDGE_WEIGHT = 1.0
NEWTON_STEPS = 8

F32 = jnp.float32
BF16 = jnp.bfloat16
I32 = jnp.int32
MESH = pl.DeviceIdType.MESH
HI = lax.Precision.HIGHEST
VMEM = pl.BlockSpec(memory_space=pltpu.VMEM)
SMEM = pl.BlockSpec(memory_space=pltpu.SMEM)
ANY = pl.BlockSpec(memory_space=pl.ANY)
DMA = pltpu.SemaphoreType.DMA
VLIM = 60 * 1024 * 1024


def dot_t(a, b, precision=None):
    return lax.dot_general(
        a, b, (((1,), (1,)), ((), ())), precision=precision, preferred_element_type=F32
    )


def coords():
    d = lax.axis_index("docs")
    core = lax.rem(d, NC)
    chip = d // NC
    return chip // NZ, lax.rem(chip, NZ), core, lax.axis_index("terms")


def dev(x, z, core, y):
    return {"docs": (x * NZ + z) * NC + core, "terms": y}


def params(collective_id=None):
    return pltpu.CompilerParams(
        collective_id=collective_id,
        has_side_effects=collective_id is not None,
        vmem_limit_bytes=VLIM,
    )


def order_kernel(ids_ref, v_ref, lab_ref, x_ref, m_ref, c_ref):
    pairs = v_ref.shape[0]
    slots = pairs // lab_ref.shape[0]
    lane = lax.broadcasted_iota(I32, (1, 128), 1)

    def step(p, carry):
        block = ids_ref[p]
        owner = block // BLK_OWN
        tile = p // slots
        code = lax.rem(block, BLK_OWN) * lab_ref.shape[0] + tile
        x_ref[owner] = v_ref[p]
        m_ref[owner] = jnp.where(lane == 64, code, lab_ref[tile])
        return carry

    lax.fori_loop(0, pairs, step, 0)


def order_blocks(values, ids, labels):
    pairs = values.shape[0]

    def kernel(ids_ref, v_ref, lab_ref, x_ref, m_ref):
        order_kernel(ids_ref, v_ref, lab_ref, x_ref, m_ref, None)

    return pl.pallas_call(
        kernel,
        out_shape=(
            jax.ShapeDtypeStruct(values.shape, BF16),
            jax.ShapeDtypeStruct((pairs, 1, 128), I32),
        ),
        in_specs=[SMEM, VMEM, VMEM],
        out_specs=(VMEM, VMEM),
        compiler_params=params(),
        name="order_blocks",
    )(ids, values, labels)


def exchange_kernel(x_ref, m_ref, ox_ref, om_ref, sx, rx, sm, rm, lsem):
    n = x_ref.shape[0]
    me = lax.axis_index("docs")
    barrier = pltpu.get_barrier_semaphore()

    def greet(i, carry):
        peer = lax.rem(me + i, n)
        pl.semaphore_signal(barrier, inc=1, device_id={"docs": peer}, device_id_type=MESH)
        return carry

    lax.fori_loop(1, n, greet, 0)
    own_x = pltpu.make_async_copy(x_ref.at[me], ox_ref.at[me], lsem.at[0])
    own_m = pltpu.make_async_copy(m_ref.at[me], om_ref.at[me], lsem.at[1])
    own_x.start()
    own_m.start()
    pl.semaphore_wait(barrier, n - 1)

    def copies(peer, slot):
        one = pltpu.make_async_remote_copy(
            src_ref=x_ref.at[peer], dst_ref=ox_ref.at[slot],
            send_sem=sx.at[peer], recv_sem=rx.at[slot],
            device_id={"docs": peer}, device_id_type=MESH,
        )
        two = pltpu.make_async_remote_copy(
            src_ref=m_ref.at[peer], dst_ref=om_ref.at[slot],
            send_sem=sm.at[peer], recv_sem=rm.at[slot],
            device_id={"docs": peer}, device_id_type=MESH,
        )
        return one, two

    def send(i, carry):
        one, two = copies(lax.rem(me + i, n), me)
        two.start()
        one.start()
        return carry

    lax.fori_loop(1, n, send, 0)
    own_x.wait()
    own_m.wait()

    def finish(i, carry):
        peer = lax.rem(me + i, n)
        one, two = copies(peer, peer)
        one.wait_recv()
        two.wait_recv()
        one.wait_send()
        two.wait_send()
        return carry

    lax.fori_loop(1, n, finish, 0)


def exchange(x, m):
    n = x.shape[0]
    return pl.pallas_call(
        exchange_kernel,
        out_shape=(jax.ShapeDtypeStruct(x.shape, x.dtype), jax.ShapeDtypeStruct(m.shape, m.dtype)),
        in_specs=[VMEM, VMEM],
        out_specs=(VMEM, VMEM),
        scratch_shapes=[DMA((n,)), DMA((n,)), DMA((n,)), DMA((n,)), DMA((2,))],
        compiler_params=params(0),
        name="exchange_blocks",
    )(x, m)


def sums_kernel(tiles, code_ref, x_ref, m_ref, sums_ref, sq_ref):
    n, rows, _ = x_ref.shape
    sums_ref[...] = jnp.zeros_like(sums_ref)
    cluster = lax.broadcasted_iota(I32, (K, rows), 0)

    def step(a, carry):
        hot = jnp.where(cluster == m_ref[a][:, :rows], 1.0, 0.0).astype(BF16)
        part = jnp.dot(hot, x_ref[a], preferred_element_type=F32)
        block = code_ref[a] // tiles
        sums_ref[block] += part
        return carry

    lax.fori_loop(0, n, step, 0)

    def square(c, total):
        s = sums_ref[c]
        return total + s * s

    total = lax.fori_loop(0, sums_ref.shape[0], square, jnp.zeros((K, 128), F32))
    sq_ref[...] = dot_t(jnp.ones((8, 128), F32), total, HI)[:1]


def own_sums(tiles, code, x, m):
    return pl.pallas_call(
        functools.partial(sums_kernel, tiles),
        out_shape=(
            jax.ShapeDtypeStruct((BLK_OWN, K, 128), F32),
            jax.ShapeDtypeStruct((1, K), F32),
        ),
        in_specs=[SMEM, VMEM, VMEM],
        out_specs=(VMEM, VMEM),
        compiler_params=params(),
        name="own_sums",
    )(code, x, m)


def norm_kernel(ny, sq_ref, scale_ref, slots, zslots, stage, ssem, rsem, zssem, zrsem):
    x, z, core, y = coords()
    group = NX * ny * NC
    me = (x * ny + y) * NC + core
    barrier = pltpu.get_barrier_semaphore()

    def member(g):
        return dev(g // (ny * NC), z, lax.rem(g, NC), lax.rem(g // NC, ny))

    def greet(i, carry):
        pl.semaphore_signal(
            barrier, inc=1, device_id=member(lax.rem(me + i, group)), device_id_type=MESH
        )
        return carry

    lax.fori_loop(1, group, greet, 0)
    for i in range(1, NZ):
        pl.semaphore_signal(
            barrier, inc=1, device_id=dev(x, lax.rem(z + i, NZ), core, y), device_id_type=MESH
        )
    slots[me] = sq_ref[...]
    pl.semaphore_wait(barrier, group - 1 + NZ - 1)

    def copy(peer, slot):
        return pltpu.make_async_remote_copy(
            src_ref=sq_ref, dst_ref=slots.at[slot],
            send_sem=ssem.at[peer], recv_sem=rsem.at[slot],
            device_id=member(peer), device_id_type=MESH,
        )

    def send(i, carry):
        copy(lax.rem(me + i, group), me).start()
        return carry

    lax.fori_loop(1, group, send, 0)

    def finish(i, carry):
        peer = lax.rem(me + i, group)
        done = copy(peer, peer)
        done.wait_recv()
        done.wait_send()
        return carry

    lax.fori_loop(1, group, finish, 0)
    total = jnp.sum(slots[...], axis=0)
    stage[...] = total
    zslots[z] = total

    def zcopy(peer, slot):
        return pltpu.make_async_remote_copy(
            src_ref=stage, dst_ref=zslots.at[slot],
            send_sem=zssem.at[peer], recv_sem=zrsem.at[slot],
            device_id=dev(x, peer, core, y), device_id_type=MESH,
        )

    for i in range(1, NZ):
        zcopy(lax.rem(z + i, NZ), z).start()
    for i in range(1, NZ):
        peer = lax.rem(z + i, NZ)
        done = zcopy(peer, peer)
        done.wait_recv()
        done.wait_send()
    scale_ref[...] = lax.rsqrt(jnp.sum(zslots[...], axis=0) + EPSILON)


def norm_scale(ny, sq):
    group = NX * ny * NC
    return pl.pallas_call(
        functools.partial(norm_kernel, ny),
        out_shape=jax.ShapeDtypeStruct((1, K), F32),
        in_specs=[VMEM],
        out_specs=VMEM,
        scratch_shapes=[
            pltpu.VMEM((group, 1, K), F32),
            pltpu.VMEM((NZ, 1, K), F32),
            pltpu.VMEM((1, K), F32),
            DMA((group,)), DMA((group,)), DMA((NZ,)), DMA((NZ,)),
        ],
        compiler_params=params(1),
        name="norm_scale",
    )(sq)


def axis_peers(ny):
    x, z, core, y = coords()
    peers = {
        "c": [dev(x, z, lax.rem(core + i, NC), y) for i in range(1, NC)],
        "x": [dev(lax.rem(x + i, NX), z, core, y) for i in range(1, NX)],
        "z": [dev(x, lax.rem(z + i, NZ), core, y) for i in range(1, NZ)],
        "y": [dev(x, z, core, lax.rem(y + i, ny)) for i in range(1, ny)],
    }
    return (x, z, core, y), peers


def greet_axes(peers):
    barrier = pltpu.get_barrier_semaphore()
    count = 0
    for axis in "cyxz":
        for peer in peers[axis]:
            pl.semaphore_signal(barrier, inc=1, device_id=peer, device_id_type=MESH)
            count += 1
    return barrier, count


def spread(pos, size, peers, source, target, ssem, rsem):
    def copy(i, send):
        p = lax.rem(pos + i, size)
        return pltpu.make_async_remote_copy(
            src_ref=source(p), dst_ref=target(pos if send else p),
            send_sem=ssem.at[p], recv_sem=rsem.at[pos if send else p],
            device_id=peers[i - 1], device_id_type=MESH,
        )

    for i in range(1, size):
        copy(i, True).start()

    def finish():
        for i in range(1, size):
            done = copy(i, False)
            done.wait_recv()
            done.wait_send()

    return finish


def gram_kernel(ny, sums_ref, scale_ref, out_ref, part, rc, a1, ry, a2, rx, a3, rz,
                cs, cr, ys, yr, xs, xr, zs, zr, xs2, xr2, ys2, yr2, cs2, cr2):
    (x, z, core, y), peers = axis_peers(ny)
    barrier, count = greet_axes(peers)
    blocks = part.shape[0]
    half = blocks // NC
    quarter = half // ny
    rows = part.shape[1]

    scale = jnp.broadcast_to(scale_ref[...], (128, K)).T
    part[...] = jnp.zeros_like(part)
    chunk = 4 if sums_ref.shape[0] % 4 == 0 else 1

    def step(i, carry):
        pieces = [(sums_ref[i * chunk + j] * scale).astype(BF16) for j in range(chunk)]
        c = jnp.concatenate(pieces, axis=1)
        part[...] += dot_t(c, c).reshape(part.shape)
        return carry

    lax.fori_loop(0, sums_ref.shape[0] // chunk, step, 0)
    pl.semaphore_wait(barrier, count)

    finish = spread(core, NC, peers["c"],
                    lambda p: part.at[pl.ds(p * half, half)], lambda p: rc, cs, cr)
    finish()
    a1[...] = part[pl.ds(core * half, half)] + rc[...]
    finish = spread(y, ny, peers["y"],
                    lambda p: a1.at[pl.ds(p * quarter, quarter)], lambda p: ry.at[p], ys, yr)
    ry[y] = a1[pl.ds(y * quarter, quarter)]
    finish()
    total = ry[0]
    for i in range(1, ny):
        total = total + ry[i]
    a2[...] = total
    finish = spread(x, NX, peers["x"], lambda p: a2.at[p], lambda p: rx.at[p], xs, xr)
    rx[x] = a2[x]
    finish()
    total = rx[0]
    for i in range(1, NX):
        total = total + rx[i]
    a3[...] = total
    rz[z] = total
    spread(z, NZ, peers["z"], lambda p: a3, lambda p: rz.at[p], zs, zr)()
    total = rz[0]
    for i in range(1, NZ):
        total = total + rz[i]
    base = core * half + y * quarter
    out_ref[base + x] = total
    spread(x, NX, peers["x"], lambda p: out_ref.at[base + x],
           lambda p: out_ref.at[base + p], xs2, xr2)()
    spread(y, ny, peers["y"], lambda p: out_ref.at[pl.ds(base, quarter)],
           lambda p: out_ref.at[pl.ds(core * half + p * quarter, quarter)], ys2, yr2)()
    spread(core, NC, peers["c"], lambda p: out_ref.at[pl.ds(core * half, half)],
           lambda p: out_ref.at[pl.ds(p * half, half)], cs2, cr2)()


def gram_sum(ny, sums, scale):
    rows = K // (NC * ny * NX)
    blocks = K // rows
    half, quarter = blocks // NC, blocks // (NC * ny)
    sems = []
    for size in (NC, ny, NX, NZ, NX, ny, NC):
        sems += [DMA((size,)), DMA((size,))]
    out = pl.pallas_call(
        functools.partial(gram_kernel, ny),
        out_shape=jax.ShapeDtypeStruct((blocks, rows, K), F32),
        in_specs=[VMEM, VMEM],
        out_specs=VMEM,
        scratch_shapes=[
            pltpu.VMEM((blocks, rows, K), F32),
            pltpu.VMEM((half, rows, K), F32),
            pltpu.VMEM((half, rows, K), F32),
            pltpu.VMEM((ny, quarter, rows, K), F32),
            pltpu.VMEM((quarter, rows, K), F32),
            pltpu.VMEM((NX, rows, K), F32),
            pltpu.VMEM((rows, K), F32),
            pltpu.VMEM((NZ, rows, K), F32),
        ] + sems,
        compiler_params=params(2),
        name="gram_sum",
    )(sums, scale)
    return out.reshape(K, K)


def block_inverse(d):
    n = d.shape[0]
    eye = (lax.broadcasted_iota(I32, (n, n), 0) == lax.broadcasted_iota(I32, (n, n), 1)).astype(F32)
    trace = jnp.sum(d * eye)
    widest = jnp.max(jnp.sum(jnp.abs(d), axis=1, keepdims=True))
    bound = jnp.minimum(trace, widest)
    low = 1.0 / bound
    inv = eye * (1.0 / bound)
    for _ in range(NEWTON_STEPS):
        inv = inv * (2.0 / (1.0 + low))
        left = jnp.dot(d, inv, precision=HI, preferred_element_type=F32)
        inv = 2.0 * inv - jnp.dot(inv, left, precision=HI, preferred_element_type=F32)
        low = 4.0 * low / ((1.0 + low) * (1.0 + low))
    left = jnp.dot(d, inv, precision=HI, preferred_element_type=F32)
    return 2.0 * inv - jnp.dot(inv, left, precision=HI, preferred_element_type=F32)


def inverse_kernel(g_ref, a_ref):
    n = 128
    steps = K // n
    eye = (lax.broadcasted_iota(I32, (K, K), 0) == lax.broadcasted_iota(I32, (K, K), 1)).astype(F32)
    a_ref[...] = g_ref[...] + RIDGE_WEIGHT * eye
    for p in range(steps):
        cut = slice(p * n, (p + 1) * n)
        inv = block_inverse(a_ref[cut, cut])
        row = jnp.dot(inv, a_ref[cut, :], precision=HI, preferred_element_type=F32)
        col = a_ref[:, cut]
        for q in range(steps):
            if q == p:
                continue
            rest = slice(q * n, (q + 1) * n)
            c = col[rest]
            a_ref[rest, :] -= jnp.dot(c, row, precision=HI, preferred_element_type=F32)
            a_ref[rest, cut] = -jnp.dot(c, inv, precision=HI, preferred_element_type=F32)
        a_ref[cut, :] = row
        a_ref[cut, cut] = inv


def ridge_inverse(gram):
    return pl.pallas_call(
        inverse_kernel,
        out_shape=jax.ShapeDtypeStruct((K, K), F32),
        in_specs=[VMEM],
        out_specs=VMEM,
        compiler_params=params(),
        name="ridge_inverse",
    )(gram)


def scores_kernel(tiles, parts, width, *refs):
    first_ref, scale_ref = refs[0], refs[1]
    groups = [refs[2 + 3 * g: 5 + 3 * g] for g in range(len(parts))]
    out_ref, sums_ref, con_ref = refs[2 + 3 * len(parts):]
    rows = groups[0][1].shape[1]
    sums_ref[...] = jnp.zeros_like(sums_ref)
    out_ref[...] = jnp.zeros_like(out_ref)
    cluster = lax.broadcasted_iota(I32, (width, rows), 0) + first_ref[0]

    for (start, count, base), (code_ref, x_ref, m_ref) in zip(parts, groups):
        def add(i, carry):
            spots, sums = [], []
            for u in range(2):
                a = start + 2 * i + u
                hot = jnp.where(cluster == m_ref[a][:, :rows], 1.0, 0.0).astype(BF16)
                sums.append(jnp.dot(hot, x_ref[2 * i + u], preferred_element_type=F32))
                spots.append(code_ref[a] // tiles + base)
            for spot, part in zip(spots, sums):
                sums_ref[spot] += part
            return carry

        lax.fori_loop(0, count // 2, add, 0)

    scale = jnp.broadcast_to(scale_ref[...], (128, width)).T

    def normalise(b, carry):
        con_ref[b] = (sums_ref[b] * scale).astype(BF16)
        return carry

    lax.fori_loop(0, sums_ref.shape[0], normalise, 0)

    for (start, count, base), (code_ref, x_ref, m_ref) in zip(parts, groups):
        def score(i, carry):
            spots, values = [], []
            for u in range(2):
                a = start + 2 * i + u
                code = code_ref[a]
                values.append(dot_t(x_ref[2 * i + u], con_ref[code // tiles + base]))
                spots.append((a, lax.rem(code, tiles)))
            for (a, tile), value in zip(spots, values):
                out_ref[a, tile] += value
            return carry

        lax.fori_loop(0, count // 2, score, 0)


def partial_scores(tiles, first, scale, parts, arrays):
    n = arrays[0][2].shape[0]
    rows = arrays[0][1].shape[1]
    width = scale.shape[1]
    ny = K // width
    flat = [a for group in arrays for a in group]
    return pl.pallas_call(
        functools.partial(scores_kernel, tiles, parts, width),
        out_shape=jax.ShapeDtypeStruct((n, tiles, rows, width), F32),
        in_specs=[SMEM, VMEM] + [SMEM, VMEM, VMEM] * len(parts),
        out_specs=VMEM,
        scratch_shapes=[
            pltpu.VMEM((ny * BLK_OWN, width, 128), F32),
            pltpu.VMEM((ny * BLK_OWN, width, 128), BF16),
        ],
        compiler_params=params(),
        name="partial_scores",
    )(first, scale, *flat)


def scatter_kernel(ny, s_ref, out_ref, rc, acc, rx, a2, rz, lsem,
                   cs, cr, xs, xr, zs, zr, ys, yr):
    (x, z, core, y), peers = axis_peers(ny)
    barrier, count = greet_axes(peers)
    width = rc.shape[-1]
    order = [lax.rem(x + i, NX) for i in range(1, NX)] + [x]
    own = []
    for i, p in enumerate(order):
        copy = pltpu.make_async_copy(s_ref.at[p, :, core], acc.at[p], lsem.at[i])
        copy.start()
        own.append(copy)
    pl.semaphore_wait(barrier, count)
    swap = []
    for i, p in enumerate(order):
        copy = pltpu.make_async_remote_copy(
            src_ref=s_ref.at[p, :, NC - 1 - core], dst_ref=rc.at[p],
            send_sem=cs.at[i], recv_sem=cr.at[i],
            device_id=peers["c"][0], device_id_type=MESH,
        )
        copy.start()
        swap.append(copy)
    sent = []
    for i, p in enumerate(order):
        own[i].wait()
        swap[i].wait_recv()
        acc[p] += rc[p]
        if i < NX - 1:
            copy = pltpu.make_async_remote_copy(
                src_ref=acc.at[p], dst_ref=rx.at[x],
                send_sem=xs.at[i], recv_sem=xr.at[x],
                device_id=peers["x"][i], device_id_type=MESH,
            )
            copy.start()
            sent.append(copy)
    a2[...] = acc[x]
    for i in range(1, NX):
        p = lax.rem(x + i, NX)
        pltpu.make_async_remote_copy(
            src_ref=acc.at[p], dst_ref=rx.at[p],
            send_sem=xs.at[i - 1], recv_sem=xr.at[p],
            device_id=peers["x"][i - 1], device_id_type=MESH,
        ).wait_recv()
        a2[...] += rx[p]
    finish = spread(z, NZ, peers["z"], lambda p: a2.at[p], lambda p: rz.at[p], zs, zr)
    finish()
    rz[z] = a2[z]
    total = rz[0]
    for i in range(1, NZ):
        total = total + rz[i]

    def lanes(p):
        return pl.ds(pl.multiple_of(p * width, width), width)

    out_ref[:, lanes(y)] = total
    spread(y, ny, peers["y"], lambda p: out_ref.at[:, lanes(y)],
           lambda p: out_ref.at[:, lanes(p)], ys, yr)()
    for copy in swap:
        copy.wait_send()
    for copy in sent:
        copy.wait_send()


def scatter_scores(ny, partial):
    n, tiles, rows, width = partial.shape
    docs = tiles * rows
    sems = []
    for size in (NX, NX, NZ, ny):
        sems += [DMA((size,)), DMA((size,))]
    return pl.pallas_call(
        functools.partial(scatter_kernel, ny),
        out_shape=jax.ShapeDtypeStruct((docs, K), F32),
        in_specs=[ANY],
        out_specs=VMEM,
        scratch_shapes=[
            pltpu.VMEM((NX, NZ, docs, width), F32),
            pltpu.VMEM((NX, NZ, docs, width), F32),
            pltpu.VMEM((NX, NZ, docs, width), F32),
            pltpu.VMEM((NZ, docs, width), F32),
            pltpu.VMEM((NZ, docs, width), F32),
            DMA((NX,)),
        ] + sems,
        compiler_params=params(3),
        name="scatter_scores",
    )(partial.reshape(NX, NZ, NC, docs, width))


def shift(array, ny, by):
    return lax.ppermute(array, "terms", [(i, (i + by) % ny) for i in range(ny)])


def body(values, block_ids, assignment):
    tiles, slots, rows, block_width = values.shape
    ny = lax.axis_size("terms")
    pairs = tiles * slots
    width = K // ny
    y = lax.axis_index("terms")
    labels = jnp.pad(
        assignment.reshape(tiles, 1, rows), ((0, 0), (0, 0), (0, 128 - rows)), constant_values=-1
    )
    ordered, meta = order_blocks(
        values.reshape(pairs, rows, block_width), block_ids.reshape(pairs), labels
    )
    own_x, own_m = exchange(ordered, meta)

    def code_of(m):
        return m[:, 0, rows]

    half = pairs // 2
    arrays, parts = [(code_of(own_m), own_x, own_m)], [(0, pairs, 0)]
    up_x, down_x = shift(own_x, ny, 1), shift(own_x, ny, -1)
    up_m = shift(own_m, ny, 1)
    arrays.append((code_of(up_m), up_x, up_m))
    parts.append((0, pairs, BLK_OWN))
    if ny > 2:
        down_m, far_m = shift(own_m, ny, -1), shift(own_m, ny, 2)
        far_a = shift(up_x[:half], ny, 1)
        far_b = shift(down_x[half:], ny, -1)
        arrays.append((code_of(down_m), down_x, down_m))
        parts.append((0, pairs, 3 * BLK_OWN))
        arrays.append((code_of(far_m), far_a, far_m))
        parts.append((0, half, 2 * BLK_OWN))
        arrays.append((code_of(far_m), far_b, far_m))
        parts.append((half, half, 2 * BLK_OWN))

    sums, sq = own_sums(tiles, code_of(own_m), own_x, own_m)
    scale = norm_scale(ny, sq)
    first = (y * width).reshape(1)
    scale_here = lax.dynamic_slice_in_dim(scale, y * width, width, 1)
    partial = partial_scores(tiles, first, scale_here, tuple(parts), arrays)
    gram = gram_sum(ny, sums, scale)
    inverse = ridge_inverse(gram)
    scores = scatter_scores(ny, partial)
    inverse_cols = lax.dynamic_slice_in_dim(inverse, y * width, width, 1)
    return jnp.dot(scores, inverse_cols, precision=HI, preferred_element_type=F32)


def solution(mesh):
    in_specs = (P("docs", "terms", None, None), P("docs", "terms"), P("docs", None))
    out_specs = P("docs", "terms")
    return jax.shard_map(body, mesh=mesh, in_specs=in_specs, out_specs=out_specs, check_vma=False)
```

time: 821 us -> 333 us (0.41)
  waiting for transfers between devices: 337 us -> 19.9 us
  Pallas kernels: 0 us -> 283 us
  blocking collectives: 186 us -> 0 us
  other arithmetic: 135 us -> 1.34 us
  matrix products: 62.6 us -> 2.36 us
  local copies, waits for them, and re-layouts: 52.6 us -> 14.8 us
  between operations: 17.9 us -> 0.1 us
  starting transfers between devices: 21.5 us -> 10.9 us
    psum x2 -> x0, waiting for transfers between devices: 337 us -> none  [the longest x1 293 us: body(): gram_matrix = lax.psum(gram_part, ('docs', 'terms'))]
    pallas_call x0 -> x8, Pallas kernels: none -> 283 us  [the longest x1 90.2 us: scatter_scores(): pl.pallas_call(functools.partial(scatter_kernel, ny), out_shape=jax.Shape...]
    another operation x18 -> x0, other arithmetic: 120 us -> none  [the longest x15 79.6 us: body(): factor = jnp.linalg.cholesky(gram_matrix + RIDGE_WEIGHT * identity)]
    all_gather x2 -> x0, blocking collectives: 109 us -> none  [the longest x1 67.7 us: body(): lax.all_gather(block_ids, 'docs', axis=0, tiled=True)]
    psum x1 -> x0, blocking collectives: 77.1 us -> none  [body(): sq_total = lax.psum(jnp.sum(sums_own * sums_own, axis=1), ('docs', 'terms'))]
    dot_general x5 -> x1, matrix products: 47.8 us -> 2.36 us  [body(): jnp.dot(scores, inverse_cols, precision=HI, preferred_element_type=F32)]
    all_to_all x2 -> x0, starting transfers between devices: 21.2 us -> none  [the longest x1 12 us: body(): lax.all_to_all(outgoing, 'docs', split_axis=0, concat_axis=0, tiled=True)]
    gather x7 -> x0, local copies, waits for them, and re-layouts: 20 us -> none  [the longest x1 8.9 us: body(): reply.reshape(pairs, K, block_width)[own_target]]
  transfers between devices with their start and end apart: 4 -> 7, of which waited for: 2 -> 1; matrix products, arithmetic and copies ran while one was open for 22% -> 3% of each run, Pallas kernels for 0% -> 30%
where the time goes in v1:
time: 333 us; the launch traced here: 332 us
  Pallas kernels  283 us (85%)
  waiting for transfers between devices  19.9 us (6%)
  local copies, waits for them, and re-layouts  14.8 us (4%)
  starting transfers between devices  10.9 us (3%)
    pallas_call x1, Pallas kernels, scatter_scores(): pl.pallas_call(functools.partial(scatter_kernel, ny), out_shape=jax.Shape...  90.2 us
    pallas_call x1, Pallas kernels, partial_scores(): pl.pallas_call(functools.partial(scores_kernel, tiles, parts, width), out...  48.9 us
    pallas_call x1, Pallas kernels, gram_sum(): pl.pallas_call(functools.partial(gram_kernel, ny), out_shape=jax.ShapeDty...  42.8 us
    pallas_call x1, Pallas kernels, exchange(): pl.pallas_call(exchange_kernel, out_shape=(jax.ShapeDtypeStruct(x.shape,...  39.2 us
    pallas_call x1, Pallas kernels, ridge_inverse(): pl.pallas_call(inverse_kernel, out_shape=jax.ShapeDtypeStruct((K, K), F32...  23.4 us
    ppermute x7, waiting for transfers between devices, shift(): return lax.ppermute(array, 'terms', [(i, (i + by) % ny) for i in range(ny)])  19.9 us
    pallas_call x1, Pallas kernels, norm_scale(): pl.pallas_call(functools.partial(norm_kernel, ny), out_shape=jax.ShapeDty...  17.6 us
    pallas_call x1, Pallas kernels, own_sums(): pl.pallas_call(functools.partial(sums_kernel, tiles), out_shape=(jax.Shap...  17.4 us
  transfers between devices with their start and end apart: 7, of which 1 were waited for; matrix products, arithmetic and copies ran while one was open for 3% of the time, Pallas kernels for 30%

profile of v1, /device:TPU:2, one launch (start us, length us, event | category | flops | bytes accessed | tf_op | source)
XLA Modules:
  0.0 332.2 jit_solution(17586849604040070739)
XLA Ops:
  0.0 1.2 reshape.19.ids_ref
  1.2 0.5 broadcast.9
  1.8 1.3 reduce.11
  3.1 0.1 reshape.21
  3.2 0.6 pad.4.lab_ref
  3.8 3.3 order_blocks.1
  7.0 39.2 %exchange_blocks.1 = (bf16[64,64,128]{2,1,0:T(8,128)(2,1)}, s32[64,1,128]{2,1,0:T(1,128)}) custom-call(bf16[64,64,128]{2,1,0:T(8,128)(2,1)} %get-tuple-element.11.x_ref, s32[64,1,128]{2,1,0:T(1,128)} %get-tuple-element.12.m_ref), custom_call_target="tpu_custom_call" | custom-call | tf_op jit(solution)/shard_map/exchange_blocks/pallas_call | solution.py:146
  46.2 3.1 collective-permute-start.3
  49.3 0.0 collective-permute-start.1
  49.3 2.2 collective-permute-start.4
  51.5 1.1 collective-permute-start.2
  52.6 1.0 collective-permute-start
  53.6 19.8 %collective-permute-done.3.refs_9_ = bf16[64,64,128]{2,1,0:T(8,128)(2,1)S(1)} collective-permute-done((bf16[64,64,128]{2,1,0:T(8,128)(2,1)}, bf16[64,64,128]{2,1,0:T(8,128)(2,1)S(1)}, u32[]{:S(2)}, u32[]{:S(2)}) %collective-permute-start.3) | collective-permute-done | bytes 1048608 | tf_op jit(solution)/shard_map/ppermute | solution.py:604
  73.4 0.0 copy-start
  73.4 0.9 slice.30
  74.3 3.6 %collective-permute-start.6 = (bf16[32,64,128]{2,1,0:T(8,128)(2,1)}, bf16[32,64,128]{2,1,0:T(8,128)(2,1)S(1)}, u32[]{:S(2)}, u32[]{:S(2)}) collective-permute-start(bf16[32,64,128]{2,1,0:T(8,128)(2,1)} %slice.30), channel_id=1, source_target_pairs={{0,3},{1,0},{2,1},{3,2},{4,7},{5,4},{6,5},{7,6},{8,11},{9,8},{10,9... | collective-permute-start | bytes 1572872 | tf_op jit(solution)/shard_map/ppermute | solution.py:604
  77.9 0.0 collective-permute-done.1.refs_6_
  77.9 0.0 copy-start.1
  77.9 0.9 slice.29
  78.8 0.0 collective-permute-start.5
  78.8 2.6 slice_reduce_fusion.3.code_ref.refs_2_
  81.4 17.4 %own_sums.1 = (f32[32,512,128]{2,1,0:T(8,128)}, f32[1,512]{1,0:T(1,128)}) custom-call(s32[64]{0:T(128)} %slice_reduce_fusion.3.code_ref.refs_2_, bf16[64,64,128]{2,1,0:T(8,128)(2,1)} %get-tuple-element.14.x_ref.refs_3_, s32[64,1,128]{2,1,0:T(1,128)} %get-tuple-element.13.m_ref.refs_4_), custom_call_target="tpu_custom_call" | custom-call | tf_op jit(solution)/shard_map/own_sums/pallas_call | solution.py:180
  98.8 17.6 %norm_scale.1.scale_ref = f32[1,512]{1,0:T(1,128)} custom-call(f32[1,512]{1,0:T(1,128)} %get-tuple-element.15.sq_ref), custom_call_target="tpu_custom_call" | custom-call | tf_op jit(solution)/shard_map/norm_scale/pallas_call | solution.py:260
  116.4 1.2 constant_dynamic-slice_fusion.refs_1_
  117.6 42.8 %gram_sum.1 = f32[32,16,512]{2,1,0:T(8,128)} custom-call(f32[32,512,128]{2,1,0:T(8,128)} %get-tuple-element.16.sums_ref, f32[1,512]{1,0:T(1,128)} %norm_scale.1.scale_ref), custom_call_target="tpu_custom_call" | custom-call | tf_op jit(solution)/shard_map/gram_sum/pallas_call | solution.py:381
  160.4 23.4 %ridge_inverse.1 = f32[512,512]{1,0:T(8,128)} custom-call(f32[512,512]{1,0:T(8,128)} %bitcast.7), custom_call_target="tpu_custom_call" | custom-call | tf_op jit(solution)/shard_map/ridge_inverse/pallas_call | solution.py:441
  183.9 0.0 collective-permute-done.4.refs_13_.refs_16_
  183.9 0.0 copy-start.4
  183.9 2.1 slice_reduce_fusion.refs_11_.refs_14_
  185.9 0.0 collective-permute-done.2.refs_10_
  185.9 0.0 copy-start.5
  185.9 1.8 slice_reduce_fusion.1.refs_8_
  187.8 0.0 collective-permute-done.refs_7_
  187.8 0.0 copy-start.6
  187.8 1.9 slice_reduce_fusion.2.refs_5_
  189.7 0.0 collective-permute-done.6.refs_15_
  189.7 0.0 copy-start.2
  189.7 0.0 collective-permute-done.5.refs_12_
  189.7 0.0 copy-start.3
  189.7 0.0 copy-done
  189.7 0.0 copy-done.1
  189.7 0.0 copy-done.4
  189.7 0.0 copy-done.5
  189.7 0.0 copy-done.6
  189.7 0.7 copy-done.2
  190.5 0.2 copy-done.3
  190.7 48.9 %partial_scores.1 = f32[64,4,64,128]{3,2,1,0:T(8,128)} custom-call(s32[1]{0:T(128)} %bitcast.refs_0_, f32[1,128]{1,0:T(1,128)} %constant_dynamic-slice_fusion.refs_1_, s32[64]{0:T(128)} %slice_reduce_fusion.3.code_ref.refs_2_, bf16[64,64,128]{2,1,0:T(8,128)(2,1)} %get-tuple-element.14.x_ref.refs_3_, s32[64,1,128]{2,1,0:T(1,128)} %get-tuple-element.13.m_ref.refs_4_, ...), custom_call_target="tpu_custom_call" | custom-call | tf_op jit(solution)/shard_map/partial_scores/pallas_call | solution.py:503
  239.6 90.2 %scatter_scores.1 = f32[256,512]{1,0:T(8,128)} custom-call(f32[4,8,2,256,128]{4,3,2,1,0:T(8,128)} %bitcast.6), custom_call_target="tpu_custom_call" | custom-call | tf_op jit(solution)/shard_map/scatter_scores/pallas_call | solution.py:585
  329.9 2.4 fusion
Async XLA Ops:
  46.2 27.2 %collective-permute-start.3 = (bf16[64,64,128]{2,1,0:T(8,128)(2,1)}, bf16[64,64,128]{2,1,0:T(8,128)(2,1)S(1)}, u32[]{:S(2)}, u32[]{:S(2)}) collective-permute-start(bf16[64,64,128]{2,1,0:T(8,128)(2,1)} %get-tuple-element.14.x_ref.refs_3_), channel_id=1, source_target_pairs={{0,3},{1,0},{2,1},{3,2},{4,7},{5,4},{6,5},{7,6},{8,11},{9,8},{10,9... | collective-permute-start | bytes 3145736 | tf_op jit(solution)/shard_map/ppermute | solution.py:604
  49.3 28.6 %collective-permute-start.1 = (bf16[64,64,128]{2,1,0:T(8,128)(2,1)}, bf16[64,64,128]{2,1,0:T(8,128)(2,1)S(1)}, u32[]{:S(2)}, u32[]{:S(2)}) collective-permute-start(bf16[64,64,128]{2,1,0:T(8,128)(2,1)} %get-tuple-element.14.x_ref.refs_3_), channel_id=1, source_target_pairs={{0,1},{1,2},{2,3},{3,0},{4,5},{5,6},{6,7},{7,4},{8,9},{9,10},{10,1... | collective-permute-start | bytes 3145736 | tf_op jit(solution)/shard_map/ppermute | solution.py:604
  49.3 134.5 %collective-permute-start.4 = (s32[64,1,128]{2,1,0:T(1,128)}, s32[64,1,128]{2,1,0:T(1,128)S(1)}, u32[]{:S(2)}, u32[]{:S(2)}) collective-permute-start(s32[64,1,128]{2,1,0:T(1,128)} %get-tuple-element.13.m_ref.refs_4_), channel_id=1, source_target_pairs={{0,2},{1,3},{2,0},{3,1},{4,6},{5,7},{6,4},{7,5},{8,10},{9,11},{10,... | collective-permute-start | bytes 98312 | tf_op jit(solution)/shard_map/ppermute | solution.py:604
  51.5 134.4 %collective-permute-start.2 = (s32[64,1,128]{2,1,0:T(1,128)}, s32[64,1,128]{2,1,0:T(1,128)S(1)}, u32[]{:S(2)}, u32[]{:S(2)}) collective-permute-start(s32[64,1,128]{2,1,0:T(1,128)} %get-tuple-element.13.m_ref.refs_4_), channel_id=1, source_target_pairs={{0,3},{1,0},{2,1},{3,2},{4,7},{5,4},{6,5},{7,6},{8,11},{9,8},{10,9... | collective-permute-start | bytes 98312 | tf_op jit(solution)/shard_map/ppermute | solution.py:604
  52.6 135.2 %collective-permute-start = (s32[64,1,128]{2,1,0:T(1,128)}, s32[64,1,128]{2,1,0:T(1,128)S(1)}, u32[]{:S(2)}, u32[]{:S(2)}) collective-permute-start(s32[64,1,128]{2,1,0:T(1,128)} %get-tuple-element.13.m_ref.refs_4_), channel_id=1, source_target_pairs={{0,1},{1,2},{2,3},{3,0},{4,5},{5,6},{6,7},{7,4},{8,9},{9,10},{10,1... | collective-permute-start | bytes 98312 | tf_op jit(solution)/shard_map/ppermute | solution.py:604
  73.4 116.3 %copy-start = (bf16[64,64,128]{2,1,0:T(8,128)(2,1)}, bf16[64,64,128]{2,1,0:T(8,128)(2,1)S(1)}, u32[]{:S(2)}) copy-start(bf16[64,64,128]{2,1,0:T(8,128)(2,1)S(1)} %collective-permute-done.3.refs_9_) | copy-start | bytes 3145732
  74.3 115.4 %collective-permute-start.6 = (bf16[32,64,128]{2,1,0:T(8,128)(2,1)}, bf16[32,64,128]{2,1,0:T(8,128)(2,1)S(1)}, u32[]{:S(2)}, u32[]{:S(2)}) collective-permute-start(bf16[32,64,128]{2,1,0:T(8,128)(2,1)} %slice.30), channel_id=1, source_target_pairs={{0,3},{1,0},{2,1},{3,2},{4,7},{5,4},{6,5},{7,6},{8,11},{9,8},{10,9... | collective-permute-start | bytes 1572872 | tf_op jit(solution)/shard_map/ppermute | solution.py:604
  77.9 111.8 %copy-start.1 = (bf16[64,64,128]{2,1,0:T(8,128)(2,1)}, bf16[64,64,128]{2,1,0:T(8,128)(2,1)S(1)}, u32[]{:S(2)}) copy-start(bf16[64,64,128]{2,1,0:T(8,128)(2,1)S(1)} %collective-permute-done.1.refs_6_) | copy-start | bytes 3145732
  78.8 110.9 %collective-permute-start.5 = (bf16[32,64,128]{2,1,0:T(8,128)(2,1)}, bf16[32,64,128]{2,1,0:T(8,128)(2,1)S(1)}, u32[]{:S(2)}, u32[]{:S(2)}) collective-permute-start(bf16[32,64,128]{2,1,0:T(8,128)(2,1)} %slice.29), channel_id=1, source_target_pairs={{0,1},{1,2},{2,3},{3,0},{4,5},{5,6},{6,7},{7,4},{8,9},{9,10},{10,1... | collective-permute-start | bytes 1572872 | tf_op jit(solution)/shard_map/ppermute | solution.py:604
  183.9 5.8 %copy-start.4 = (s32[64,1,128]{2,1,0:T(1,128)}, s32[64,1,128]{2,1,0:T(1,128)S(1)}, u32[]{:S(2)}) copy-start(s32[64,1,128]{2,1,0:T(1,128)S(1)} %collective-permute-done.4.refs_13_.refs_16_) | copy-start | bytes 98308
  185.9 3.8 %copy-start.5 = (s32[64,1,128]{2,1,0:T(1,128)}, s32[64,1,128]{2,1,0:T(1,128)S(1)}, u32[]{:S(2)}) copy-start(s32[64,1,128]{2,1,0:T(1,128)S(1)} %collective-permute-done.2.refs_10_) | copy-start | bytes 98308
  187.8 1.9 copy-start.6
  189.7 0.8 copy-start.2
  189.7 1.0 copy-start.3

commit v2 on v1

--- a/solution.py
+++ b/solution.py
@@ -15,6 +15,7 @@
 EPSILON = 1e-06
 RIDGE_WEIGHT = 1.0
 NEWTON_STEPS = 8
+UNROLL = 4
 
 F32 = jnp.float32
 BF16 = jnp.bfloat16
@@ -43,6 +44,10 @@
 
 def dev(x, z, core, y):
     return {"docs": (x * NZ + z) * NC + core, "terms": y}
+
+
+def cost(us):
+    return pl.CostEstimate(flops=int(us * 5e8), bytes_accessed=int(us * 2e6), transcendentals=0)
 
 
 def params(collective_id=None):
@@ -159,14 +164,18 @@
     sums_ref[...] = jnp.zeros_like(sums_ref)
     cluster = lax.broadcasted_iota(I32, (K, rows), 0)
 
-    def step(a, carry):
-        hot = jnp.where(cluster == m_ref[a][:, :rows], 1.0, 0.0).astype(BF16)
-        part = jnp.dot(hot, x_ref[a], preferred_element_type=F32)
-        block = code_ref[a] // tiles
-        sums_ref[block] += part
-        return carry
-
-    lax.fori_loop(0, n, step, 0)
+    def step(i, carry):
+        spots, sums = [], []
+        for u in range(2):
+            a = 2 * i + u
+            hot = jnp.where(cluster == m_ref[a][:, :rows], 1.0, 0.0).astype(BF16)
+            sums.append(jnp.dot(hot, x_ref[a], preferred_element_type=F32))
+            spots.append(code_ref[a] // tiles)
+        for spot, part in zip(spots, sums):
+            sums_ref[spot] += part
+        return carry
+
+    lax.fori_loop(0, n // 2, step, 0)
 
     def square(c, total):
         s = sums_ref[c]
@@ -186,6 +195,7 @@
         in_specs=[SMEM, VMEM, VMEM],
         out_specs=(VMEM, VMEM),
         compiler_params=params(),
+        cost_estimate=cost(17),
         name="own_sums",
     )(code, x, m)
 
@@ -269,6 +279,7 @@
             DMA((group,)), DMA((group,)), DMA((NZ,)), DMA((NZ,)),
         ],
         compiler_params=params(1),
+        cost_estimate=cost(17),
         name="norm_scale",
     )(sq)
 
@@ -313,90 +324,6 @@
             done.wait_send()
 
     return finish
-
-
-def gram_kernel(ny, sums_ref, scale_ref, out_ref, part, rc, a1, ry, a2, rx, a3, rz,
-                cs, cr, ys, yr, xs, xr, zs, zr, xs2, xr2, ys2, yr2, cs2, cr2):
-    (x, z, core, y), peers = axis_peers(ny)
-    barrier, count = greet_axes(peers)
-    blocks = part.shape[0]
-    half = blocks // NC
-    quarter = half // ny
-    rows = part.shape[1]
-
-    scale = jnp.broadcast_to(scale_ref[...], (128, K)).T
-    part[...] = jnp.zeros_like(part)
-    chunk = 4 if sums_ref.shape[0] % 4 == 0 else 1
-
-    def step(i, carry):
-        pieces = [(sums_ref[i * chunk + j] * scale).astype(BF16) for j in range(chunk)]
-        c = jnp.concatenate(pieces, axis=1)
-        part[...] += dot_t(c, c).reshape(part.shape)
-        return carry
-
-    lax.fori_loop(0, sums_ref.shape[0] // chunk, step, 0)
-    pl.semaphore_wait(barrier, count)
-
-    finish = spread(core, NC, peers["c"],
-                    lambda p: part.at[pl.ds(p * half, half)], lambda p: rc, cs, cr)
-    finish()
-    a1[...] = part[pl.ds(core * half, half)] + rc[...]
-    finish = spread(y, ny, peers["y"],
-                    lambda p: a1.at[pl.ds(p * quarter, quarter)], lambda p: ry.at[p], ys, yr)
-    ry[y] = a1[pl.ds(y * quarter, quarter)]
-    finish()
-    total = ry[0]
-    for i in range(1, ny):
-        total = total + ry[i]
-    a2[...] = total
-    finish = spread(x, NX, peers["x"], lambda p: a2.at[p], lambda p: rx.at[p], xs, xr)
-    rx[x] = a2[x]
-    finish()
-    total = rx[0]
-    for i in range(1, NX):
-        total = total + rx[i]
-    a3[...] = total
-    rz[z] = total
-    spread(z, NZ, peers["z"], lambda p: a3, lambda p: rz.at[p], zs, zr)()
-    total = rz[0]
-    for i in range(1, NZ):
-        total = total + rz[i]
-    base = core * half + y * quarter
-    out_ref[base + x] = total
-    spread(x, NX, peers["x"], lambda p: out_ref.at[base + x],
-           lambda p: out_ref.at[base + p], xs2, xr2)()
-    spread(y, ny, peers["y"], lambda p: out_ref.at[pl.ds(base, quarter)],
-           lambda p: out_ref.at[pl.ds(core * half + p * quarter, quarter)], ys2, yr2)()
-    spread(core, NC, peers["c"], lambda p: out_ref.at[pl.ds(core * half, half)],
-           lambda p: out_ref.at[pl.ds(p * half, half)], cs2, cr2)()
-
-
-def gram_sum(ny, sums, scale):
-    rows = K // (NC * ny * NX)
-    blocks = K // rows
-    half, quarter = blocks // NC, blocks // (NC * ny)
-    sems = []
-    for size in (NC, ny, NX, NZ, NX, ny, NC):
-        sems += [DMA((size,)), DMA((size,))]
-    out = pl.pallas_call(
-        functools.partial(gram_kernel, ny),
-        out_shape=jax.ShapeDtypeStruct((blocks, rows, K), F32),
-        in_specs=[VMEM, VMEM],
-        out_specs=VMEM,
-        scratch_shapes=[
-            pltpu.VMEM((blocks, rows, K), F32),
-            pltpu.VMEM((half, rows, K), F32),
-            pltpu.VMEM((half, rows, K), F32),
-            pltpu.VMEM((ny, quarter, rows, K), F32),
-            pltpu.VMEM((quarter, rows, K), F32),
-            pltpu.VMEM((NX, rows, K), F32),
-            pltpu.VMEM((rows, K), F32),
-            pltpu.VMEM((NZ, rows, K), F32),
-        ] + sems,
-        compiler_params=params(2),
-        name="gram_sum",
-    )(sums, scale)
-    return out.reshape(K, K)
 
 
 def block_inverse(d):
@@ -416,38 +343,6 @@
     return 2.0 * inv - jnp.dot(inv, left, precision=HI, preferred_element_type=F32)
 
 
-def inverse_kernel(g_ref, a_ref):
-    n = 128
-    steps = K // n
-    eye = (lax.broadcasted_iota(I32, (K, K), 0) == lax.broadcasted_iota(I32, (K, K), 1)).astype(F32)
-    a_ref[...] = g_ref[...] + RIDGE_WEIGHT * eye
-    for p in range(steps):
-        cut = slice(p * n, (p + 1) * n)
-        inv = block_inverse(a_ref[cut, cut])
-        row = jnp.dot(inv, a_ref[cut, :], precision=HI, preferred_element_type=F32)
-        col = a_ref[:, cut]
-        for q in range(steps):
-            if q == p:
-                continue
-            rest = slice(q * n, (q + 1) * n)
-            c = col[rest]
-            a_ref[rest, :] -= jnp.dot(c, row, precision=HI, preferred_element_type=F32)
-            a_ref[rest, cut] = -jnp.dot(c, inv, precision=HI, preferred_element_type=F32)
-        a_ref[cut, :] = row
-        a_ref[cut, cut] = inv
-
-
-def ridge_inverse(gram):
-    return pl.pallas_call(
-        inverse_kernel,
-        out_shape=jax.ShapeDtypeStruct((K, K), F32),
-        in_specs=[VMEM],
-        out_specs=VMEM,
-        compiler_params=params(),
-        name="ridge_inverse",
-    )(gram)
-
-
 def scores_kernel(tiles, parts, width, *refs):
     first_ref, scale_ref = refs[0], refs[1]
     groups = [refs[2 + 3 * g: 5 + 3 * g] for g in range(len(parts))]
@@ -460,16 +355,16 @@
     for (start, count, base), (code_ref, x_ref, m_ref) in zip(parts, groups):
         def add(i, carry):
             spots, sums = [], []
-            for u in range(2):
-                a = start + 2 * i + u
+            for u in range(UNROLL):
+                a = start + UNROLL * i + u
                 hot = jnp.where(cluster == m_ref[a][:, :rows], 1.0, 0.0).astype(BF16)
-                sums.append(jnp.dot(hot, x_ref[2 * i + u], preferred_element_type=F32))
+                sums.append(jnp.dot(hot, x_ref[UNROLL * i + u], preferred_element_type=F32))
                 spots.append(code_ref[a] // tiles + base)
             for spot, part in zip(spots, sums):
                 sums_ref[spot] += part
             return carry
 
-        lax.fori_loop(0, count // 2, add, 0)
+        lax.fori_loop(0, count // UNROLL, add, 0)
 
     scale = jnp.broadcast_to(scale_ref[...], (128, width)).T
 
@@ -482,16 +377,16 @@
     for (start, count, base), (code_ref, x_ref, m_ref) in zip(parts, groups):
         def score(i, carry):
             spots, values = [], []
-            for u in range(2):
-                a = start + 2 * i + u
+            for u in range(UNROLL):
+                a = start + UNROLL * i + u
                 code = code_ref[a]
-                values.append(dot_t(x_ref[2 * i + u], con_ref[code // tiles + base]))
+                values.append(dot_t(x_ref[UNROLL * i + u], con_ref[code // tiles + base]))
                 spots.append((a, lax.rem(code, tiles)))
             for (a, tile), value in zip(spots, values):
                 out_ref[a, tile] += value
             return carry
 
-        lax.fori_loop(0, count // 2, score, 0)
+        lax.fori_loop(0, count // UNROLL, score, 0)
 
 
 def partial_scores(tiles, first, scale, parts, arrays):
@@ -510,16 +405,52 @@
             pltpu.VMEM((ny * BLK_OWN, width, 128), BF16),
         ],
         compiler_params=params(),
+        cost_estimate=cost(45),
         name="partial_scores",
     )(first, scale, *flat)
 
 
-def scatter_kernel(ny, s_ref, out_ref, rc, acc, rx, a2, rz, lsem,
-                   cs, cr, xs, xr, zs, zr, ys, yr):
+def gram_part(sums_ref, scale_ref, part):
+    scale = jnp.broadcast_to(scale_ref[...], (128, K)).T
+    part[...] = jnp.zeros_like(part)
+    chunk = 4
+
+    def step(i, carry):
+        pieces = [(sums_ref[i * chunk + j] * scale).astype(BF16) for j in range(chunk)]
+        c = jnp.concatenate(pieces, axis=1)
+        part[...] += dot_t(c, c).reshape(part.shape)
+        return carry
+
+    lax.fori_loop(0, sums_ref.shape[0] // chunk, step, 0)
+
+
+def inverse_panel(a_ref, p):
+    n = 128
+    cut = slice(p * n, (p + 1) * n)
+    inv = block_inverse(a_ref[cut, cut])
+    row = jnp.dot(inv, a_ref[cut, :], precision=HI, preferred_element_type=F32)
+    col = a_ref[:, cut]
+    for q in range(K // n):
+        if q == p:
+            continue
+        rest = slice(q * n, (q + 1) * n)
+        c = col[rest]
+        a_ref[rest, :] -= jnp.dot(c, row, precision=HI, preferred_element_type=F32)
+        a_ref[rest, cut] = -jnp.dot(c, inv, precision=HI, preferred_element_type=F32)
+    a_ref[cut, :] = row
+    a_ref[cut, cut] = inv
+
+
+def reduce_kernel(ny, s_ref, sums_ref, scale_ref, scores_ref, a_ref,
+                  rc, acc, rx, rz, lsem,
+                  part, gc, a1, gy, a2, gx, a3, gz, gram,
+                  cs, cr, xs, xr, zs, zr, ys, yr,
+                  gcs, gcr, gys, gyr, gxs, gxr, gzs, gzr,
+                  gxs2, gxr2, gys2, gyr2, gcs2, gcr2):
     (x, z, core, y), peers = axis_peers(ny)
     barrier, count = greet_axes(peers)
     width = rc.shape[-1]
-    order = [lax.rem(x + i, NX) for i in range(1, NX)] + [x]
+    order = [lax.rem(x + i, NX) for i in (NX - 1, 1, 2, 0)]
     own = []
     for i, p in enumerate(order):
         copy = pltpu.make_async_copy(s_ref.at[p, :, core], acc.at[p], lsem.at[i])
@@ -535,31 +466,90 @@
         )
         copy.start()
         swap.append(copy)
-    sent = []
-    for i, p in enumerate(order):
+
+    def pair(i):
         own[i].wait()
         swap[i].wait_recv()
-        acc[p] += rc[p]
-        if i < NX - 1:
-            copy = pltpu.make_async_remote_copy(
-                src_ref=acc.at[p], dst_ref=rx.at[x],
-                send_sem=xs.at[i], recv_sem=xr.at[x],
-                device_id=peers["x"][i], device_id_type=MESH,
-            )
-            copy.start()
-            sent.append(copy)
-    a2[...] = acc[x]
+        acc[order[i]] += rc[order[i]]
+
+    cut = NZ // 2
+    upper, lower = peers["x"][0], peers["x"][NX - 2]
+
+    def hop(s, down):
+        sent = lax.rem(x + (s + 1 if down else 2 * NX - s - 1), NX)
+        part_z = pl.ds(cut if down else 0, cut)
+        return pltpu.make_async_remote_copy(
+            src_ref=acc.at[sent, part_z], dst_ref=rx.at[s, part_z],
+            send_sem=xs.at[2 * s + down], recv_sem=xr.at[2 * s + down],
+            device_id=lower if down else upper, device_id_type=MESH,
+        )
+
+    def land(s, down):
+        hop(s, down).wait_recv()
+        got = lax.rem(x + (s + 2 if down else 2 * NX - s - 2), NX)
+        part_z = pl.ds(cut if down else 0, cut)
+        acc[got, part_z] += rx[s, part_z]
+
+    blocks = part.shape[0]
+    half = blocks // NC
+    quarter = half // ny
+
+    gram_part(sums_ref, scale_ref, part)
+    finish = spread(core, NC, peers["c"],
+                    lambda p: part.at[pl.ds(p * half, half)], lambda p: gc, gcs, gcr)
+    pair(0)
+    hop(0, 0).start()
+    pair(1)
+    hop(0, 1).start()
+    finish()
+    a1[...] = part[pl.ds(core * half, half)] + gc[...]
+    finish = spread(y, ny, peers["y"],
+                    lambda p: a1.at[pl.ds(p * quarter, quarter)], lambda p: gy.at[p], gys, gyr)
+    pair(2)
+    pair(3)
+    gy[y] = a1[pl.ds(y * quarter, quarter)]
+    finish()
+    total = gy[0]
+    for i in range(1, ny):
+        total = total + gy[i]
+    a2[...] = total
+    finish = spread(x, NX, peers["x"], lambda p: a2.at[p], lambda p: gx.at[p], gxs, gxr)
+    gx[x] = a2[x]
+    for down in range(2):
+        land(0, down)
+        hop(1, down).start()
+    finish()
+    total = gx[0]
     for i in range(1, NX):
-        p = lax.rem(x + i, NX)
-        pltpu.make_async_remote_copy(
-            src_ref=acc.at[p], dst_ref=rx.at[p],
-            send_sem=xs.at[i - 1], recv_sem=xr.at[p],
-            device_id=peers["x"][i - 1], device_id_type=MESH,
-        ).wait_recv()
-        a2[...] += rx[p]
-    finish = spread(z, NZ, peers["z"], lambda p: a2.at[p], lambda p: rz.at[p], zs, zr)
+        total = total + gx[i]
+    a3[...] = total
+    gz[z] = total
+    spread(z, NZ, peers["z"], lambda p: a3, lambda p: gz.at[p], gzs, gzr)()
+    total = gz[0]
+    for i in range(1, NZ):
+        total = total + gz[i]
+    base = core * half + y * quarter
+    gram[base + x] = total
+    finish = spread(x, NX, peers["x"], lambda p: gram.at[base + x],
+                    lambda p: gram.at[base + p], gxs2, gxr2)
+    for down in range(2):
+        land(1, down)
+        hop(2, down).start()
     finish()
-    rz[z] = a2[z]
+    spread(y, ny, peers["y"], lambda p: gram.at[pl.ds(base, quarter)],
+           lambda p: gram.at[pl.ds(core * half + p * quarter, quarter)], gys2, gyr2)()
+    spread(core, NC, peers["c"], lambda p: gram.at[pl.ds(core * half, half)],
+           lambda p: gram.at[pl.ds(p * half, half)], gcs2, gcr2)()
+
+    eye = (lax.broadcasted_iota(I32, (K, K), 0) == lax.broadcasted_iota(I32, (K, K), 1)).astype(F32)
+    a_ref[...] = gram[...].reshape(K, K) + RIDGE_WEIGHT * eye
+    for down in range(2):
+        land(2, down)
+    finish = spread(z, NZ, peers["z"], lambda p: acc.at[x, p], lambda p: rz.at[p], zs, zr)
+    for p in range(K // 128):
+        inverse_panel(a_ref, p)
+    rz[z] = acc[x, z]
+    finish()
     total = rz[0]
     for i in range(1, NZ):
         total = total + rz[i]
@@ -567,37 +557,49 @@
     def lanes(p):
         return pl.ds(pl.multiple_of(p * width, width), width)
 
-    out_ref[:, lanes(y)] = total
-    spread(y, ny, peers["y"], lambda p: out_ref.at[:, lanes(y)],
-           lambda p: out_ref.at[:, lanes(p)], ys, yr)()
+    scores_ref[:, lanes(y)] = total
+    spread(y, ny, peers["y"], lambda p: scores_ref.at[:, lanes(y)],
+           lambda p: scores_ref.at[:, lanes(p)], ys, yr)()
     for copy in swap:
         copy.wait_send()
-    for copy in sent:
-        copy.wait_send()
-
-
-def scatter_scores(ny, partial):
+    for s in range(NX - 1):
+        for down in range(2):
+            hop(s, down).wait_send()
+
+
+def reduce_scores(ny, partial, sums, scale):
     n, tiles, rows, width = partial.shape
     docs = tiles * rows
+    part_rows = K // (NC * ny * NX)
+    blocks = K // part_rows
+    half, quarter = blocks // NC, blocks // (NC * ny)
     sems = []
-    for size in (NX, NX, NZ, ny):
+    for size in (NX, 2 * (NX - 1), NZ, ny, NC, ny, NX, NZ, NX, ny, NC):
         sems += [DMA((size,)), DMA((size,))]
     return pl.pallas_call(
-        functools.partial(scatter_kernel, ny),
-        out_shape=jax.ShapeDtypeStruct((docs, K), F32),
-        in_specs=[ANY],
-        out_specs=VMEM,
+        functools.partial(reduce_kernel, ny),
+        out_shape=(jax.ShapeDtypeStruct((docs, K), F32), jax.ShapeDtypeStruct((K, K), F32)),
+        in_specs=[ANY, VMEM, VMEM],
+        out_specs=(VMEM, VMEM),
         scratch_shapes=[
             pltpu.VMEM((NX, NZ, docs, width), F32),
             pltpu.VMEM((NX, NZ, docs, width), F32),
-            pltpu.VMEM((NX, NZ, docs, width), F32),
-            pltpu.VMEM((NZ, docs, width), F32),
+            pltpu.VMEM((NX - 1, NZ, docs, width), F32),
             pltpu.VMEM((NZ, docs, width), F32),
             DMA((NX,)),
+            pltpu.VMEM((blocks, part_rows, K), F32),
+            pltpu.VMEM((half, part_rows, K), F32),
+            pltpu.VMEM((half, part_rows, K), F32),
+            pltpu.VMEM((ny, quarter, part_rows, K), F32),
+            pltpu.VMEM((quarter, part_rows, K), F32),
+            pltpu.VMEM((NX, part_rows, K), F32),
+            pltpu.VMEM((part_rows, K), F32),
+            pltpu.VMEM((NZ, part_rows, K), F32),
+            pltpu.VMEM((blocks, part_rows, K), F32),
         ] + sems,
-        compiler_params=params(3),
-        name="scatter_scores",
-    )(partial.reshape(NX, NZ, NC, docs, width))
+        compiler_params=params(2),
+        name="reduce_scores",
+    )(partial.reshape(NX, NZ, NC, docs, width), sums, scale)
 
 
 def shift(array, ny, by):
@@ -643,9 +645,7 @@
     first = (y * width).reshape(1)
     scale_here = lax.dynamic_slice_in_dim(scale, y * width, width, 1)
     partial = partial_scores(tiles, first, scale_here, tuple(parts), arrays)
-    gram = gram_sum(ny, sums, scale)
-    inverse = ridge_inverse(gram)
-    scores = scatter_scores(ny, partial)
+    scores, inverse = reduce_scores(ny, partial, sums, scale)
     inverse_cols = lax.dynamic_slice_in_dim(inverse, y * width, width, 1)
     return jnp.dot(scores, inverse_cols, precision=HI, preferred_element_type=F32)
 

time: 333 us -> 225 us (0.68)
  Pallas kernels: 283 us -> 192 us
  waiting for transfers between devices: 19.9 us -> 3.19 us
    pallas_call x3 -> x1, Pallas kernels: 156 us -> 82 us  [reduce_scores(): pl.pallas_call(functools.partial(reduce_kernel, ny), out_shape=(jax.Shape...]
    pallas_call x1, Pallas kernels: 48.9 us -> 31.8 us  [partial_scores(): pl.pallas_call(functools.partial(scores_kernel, tiles, parts, width), out...]
    ppermute x7, waiting for transfers between devices: 19.9 us -> 3.19 us  [shift(): return lax.ppermute(array, 'terms', [(i, (i + by) % ny) for i in range(ny)])]
    pallas_call x1, Pallas kernels: 17.6 us -> 21.9 us  [norm_scale(): pl.pallas_call(functools.partial(norm_kernel, ny), out_shape=jax.ShapeDty...]
    pallas_call x1, Pallas kernels: 17.4 us -> 14 us  [own_sums(): pl.pallas_call(functools.partial(sums_kernel, tiles), out_shape=(jax.Shap...]
  transfers between devices with their start and end apart: 7 -> 7, of which waited for: 1 -> 1; matrix products, arithmetic and copies ran while one was open for 3% -> 4% of each run, Pallas kernels for 30% -> 16%
where the time goes in v2:
time: 225 us; the launch traced here: 222 us
  Pallas kernels  192 us (85%)
  local copies, waits for them, and re-layouts  11.9 us (5%)
  starting transfers between devices  11.3 us (5%)
  waiting for transfers between devices  3.19 us (1%)
  matrix products  2.35 us (1%)
    pallas_call x1, Pallas kernels, reduce_scores(): pl.pallas_call(functools.partial(reduce_kernel, ny), out_shape=(jax.Shape...  82 us
    pallas_call x1, Pallas kernels, exchange(): pl.pallas_call(exchange_kernel, out_shape=(jax.ShapeDtypeStruct(x.shape,...  39.2 us
    pallas_call x1, Pallas kernels, partial_scores(): pl.pallas_call(functools.partial(scores_kernel, tiles, parts, width), out...  31.8 us
    pallas_call x1, Pallas kernels, norm_scale(): pl.pallas_call(functools.partial(norm_kernel, ny), out_shape=jax.ShapeDty...  21.9 us
    pallas_call x1, Pallas kernels, own_sums(): pl.pallas_call(functools.partial(sums_kernel, tiles), out_shape=(jax.Shap...  14 us
    ppermute x7, starting transfers between devices, shift(): return lax.ppermute(array, 'terms', [(i, (i + by) % ny) for i in range(ny)])  11.3 us
    slice x4, local copies, waits for them, and re-layouts, code_of(): return m[:, 0, rows]  8.25 us
  transfers between devices with their start and end apart: 7, of which 1 were waited for; matrix products, arithmetic and copies ran while one was open for 4% of the time, Pallas kernels for 16%

profile of v2, /device:TPU:2, one launch (start us, length us, event | category | flops | bytes accessed | tf_op | source)
XLA Modules:
  0.0 222.4 jit_solution(11972430530348584186)
XLA Ops:
  0.0 1.3 reshape.16.ids_ref
  1.3 0.5 broadcast.9
  1.8 1.3 reduce.11
  3.2 0.1 reshape.18
  3.3 0.6 pad.4.lab_ref
  3.8 3.3 %order_blocks.1 = (bf16[64,64,128]{2,1,0:T(8,128)(2,1)}, s32[64,1,128]{2,1,0:T(1,128)}) custom-call(s32[64]{0:T(128)} %reshape.16.ids_ref, bf16[64,64,128]{2,1,0:T(8,128)(2,1)} %bitcast.6, s32[4,1,128]{2,1,0:T(1,128)} %pad.4.lab_ref), custom_call_target="tpu_custom_call" | custom-call | tf_op jit(solution)/shard_map/order_blocks/pallas_call | solution.py:84
  7.1 39.2 %exchange_blocks.1 = (bf16[64,64,128]{2,1,0:T(8,128)(2,1)}, s32[64,1,128]{2,1,0:T(1,128)}) custom-call(bf16[64,64,128]{2,1,0:T(8,128)(2,1)} %get-tuple-element.13.x_ref, s32[64,1,128]{2,1,0:T(1,128)} %get-tuple-element.14.m_ref), custom_call_target="tpu_custom_call" | custom-call | tf_op jit(solution)/shard_map/exchange_blocks/pallas_call | solution.py:151
  46.3 3.1 %collective-permute-start.3 = (bf16[64,64,128]{2,1,0:T(8,128)(2,1)}, bf16[64,64,128]{2,1,0:T(8,128)(2,1)S(1)}, u32[]{:S(2)}, u32[]{:S(2)}) collective-permute-start(bf16[64,64,128]{2,1,0:T(8,128)(2,1)} %get-tuple-element.16.x_ref.refs_3_), channel_id=1, source_target_pairs={{0,3},{1,0},{2,1},{3,2},{4,7},{5,4},{6,5},{7,6},{8,11},{9,8},{10,9... | collective-permute-start | bytes 3145736 | tf_op jit(solution)/shard_map/ppermute | solution.py:606
  49.4 0.0 collective-permute-start.1
  49.4 2.2 collective-permute-start.4
  51.6 1.1 collective-permute-start.2
  52.7 1.0 collective-permute-start
  53.6 2.7 %slice_reduce_fusion.3.code_ref.refs_2_ = s32[64]{0:T(128)} fusion(s32[64,1,128]{2,1,0:T(1,128)} %get-tuple-element.15.m_ref.refs_4_), kind=kLoop, calls=%fused_computation.5 | loop fusion | bytes 512 | tf_op jit(solution)/shard_map/slice | solution.py:624
  56.3 14.0 %own_sums.1 = (f32[32,512,128]{2,1,0:T(8,128)}, f32[1,512]{1,0:T(1,128)}) custom-call(s32[64]{0:T(128)} %slice_reduce_fusion.3.code_ref.refs_2_, bf16[64,64,128]{2,1,0:T(8,128)(2,1)} %get-tuple-element.16.x_ref.refs_3_, s32[64,1,128]{2,1,0:T(1,128)} %get-tuple-element.15.m_ref.refs_4_), custom_call_target="tpu_custom_call" | custom-call | flops 8499999744 | bytes 34000000 | tf_op jit(solution)/shard_map/own_sums/pallas_call | solution.py:189
  70.3 3.2 %collective-permute-done.3.refs_9_ = bf16[64,64,128]{2,1,0:T(8,128)(2,1)S(1)} collective-permute-done((bf16[64,64,128]{2,1,0:T(8,128)(2,1)}, bf16[64,64,128]{2,1,0:T(8,128)(2,1)S(1)}, u32[]{:S(2)}, u32[]{:S(2)}) %collective-permute-start.3) | collective-permute-done | bytes 1048608 | tf_op jit(solution)/shard_map/ppermute | solution.py:606
  73.5 0.0 copy-start
  73.5 3.7 %collective-permute-start.6 = (bf16[32,64,128]{2,1,0:T(8,128)(2,1)S(1)}, bf16[32,64,128]{2,1,0:T(8,128)(2,1)}, u32[]{:S(2)}, u32[]{:S(2)}) collective-permute-start(bf16[32,64,128]{2,1,0:T(8,128)(2,1)S(1)} %slice.30), channel_id=1, source_target_pairs={{0,3},{1,0},{2,1},{3,2},{4,7},{5,4},{6,5},{7,6},{8,11},{9,8},{10,9... | collective-permute-start | bytes 1572872 | tf_op jit(solution)/shard_map/ppermute | solution.py:606
  77.2 0.0 collective-permute-done.1.refs_6_
  77.2 0.0 copy-start.1
  77.2 0.3 collective-permute-start.5
  77.5 21.9 %norm_scale.1.scale_ref = f32[1,512]{1,0:T(1,128)} custom-call(f32[1,512]{1,0:T(1,128)} %get-tuple-element.17.sq_ref), custom_call_target="tpu_custom_call" | custom-call | flops 8499999744 | bytes 34000000 | tf_op jit(solution)/shard_map/norm_scale/pallas_call | solution.py:270
  99.4 0.0 copy-done
  99.4 0.0 copy-done.1
  99.4 1.1 constant_dynamic-slice_fusion.refs_1_
  100.5 0.0 collective-permute-done.4.refs_13_.refs_16_
  100.5 0.0 copy-start.2
  100.5 1.8 slice_reduce_fusion.refs_11_.refs_14_
  102.3 0.0 collective-permute-done.2.refs_10_
  102.3 0.0 copy-start.3
  102.3 1.9 slice_reduce_fusion.1.refs_8_
  104.2 0.0 collective-permute-done.refs_7_
  104.2 0.0 copy-start.4
  104.2 1.9 slice_reduce_fusion.2.refs_5_
  106.1 0.0 collective-permute-done.6.refs_15_
  106.1 0.0 collective-permute-done.5.refs_12_
  106.1 0.0 copy-done.2
  106.1 0.0 copy-done.3
  106.1 0.0 copy-done.4
  106.2 31.8 %partial_scores.1 = f32[64,4,64,128]{3,2,1,0:T(8,128)} custom-call(s32[1]{0:T(128)} %bitcast.refs_0_, f32[1,128]{1,0:T(1,128)} %constant_dynamic-slice_fusion.refs_1_, s32[64]{0:T(128)} %slice_reduce_fusion.3.code_ref.refs_2_, bf16[64,64,128]{2,1,0:T(8,128)(2,1)} %get-tuple-element.16.x_ref.refs_3_, s32[64,1,128]{2,1,0:T(1,128)} %get-tuple-element.15.m_ref.refs_4_, ...), custom_call_target="tpu_custom_call" | custom-call | flops 22499999744 | bytes 90000000 | tf_op jit(solution)/shard_map/partial_scores/pallas_call | solution.py:398
  138.0 82.0 %reduce_scores.1 = (f32[256,512]{1,0:T(8,128)}, f32[512,512]{1,0:T(8,128)}) custom-call(f32[4,8,2,256,128]{4,3,2,1,0:T(8,128)} %bitcast.5, f32[32,512,128]{2,1,0:T(8,128)} %get-tuple-element.18.sums_ref, f32[1,512]{1,0:T(1,128)} %norm_scale.1.scale_ref), custom_call_target="tpu_custom_call" | custom-call | tf_op jit(solution)/shard_map/reduce_scores/pallas_call | solution.py:579
  220.0 2.3 %fusion = f32[256,128]{1,0:T(8,128)} fusion(f32[256,512]{1,0:T(8,128)} %get-tuple-element.19, f32[512,512]{1,0:T(8,128)} %get-tuple-element.20, s32[]{:T(128)S(6)} %select_n.4), kind=kOutput, calls=%fused_computation | convolution fusion | flops 201326592 | bytes 917508 | tf_op jit(solution)/shard_map/dot_general | solution.py:650
  (2 shorter events, 0.1 us)
Async XLA Ops:
  46.3 27.2 %collective-permute-start.3 = (bf16[64,64,128]{2,1,0:T(8,128)(2,1)}, bf16[64,64,128]{2,1,0:T(8,128)(2,1)S(1)}, u32[]{:S(2)}, u32[]{:S(2)}) collective-permute-start(bf16[64,64,128]{2,1,0:T(8,128)(2,1)} %get-tuple-element.16.x_ref.refs_3_), channel_id=1, source_target_pairs={{0,3},{1,0},{2,1},{3,2},{4,7},{5,4},{6,5},{7,6},{8,11},{9,8},{10,9... | collective-permute-start | bytes 3145736 | tf_op jit(solution)/shard_map/ppermute | solution.py:606
  49.4 27.8 %collective-permute-start.1 = (bf16[64,64,128]{2,1,0:T(8,128)(2,1)}, bf16[64,64,128]{2,1,0:T(8,128)(2,1)S(1)}, u32[]{:S(2)}, u32[]{:S(2)}) collective-permute-start(bf16[64,64,128]{2,1,0:T(8,128)(2,1)} %get-tuple-element.16.x_ref.refs_3_), channel_id=1, source_target_pairs={{0,1},{1,2},{2,3},{3,0},{4,5},{5,6},{6,7},{7,4},{8,9},{9,10},{10,1... | collective-permute-start | bytes 3145736 | tf_op jit(solution)/shard_map/ppermute | solution.py:606
  49.4 51.1 %collective-permute-start.4 = (s32[64,1,128]{2,1,0:T(1,128)}, s32[64,1,128]{2,1,0:T(1,128)S(1)}, u32[]{:S(2)}, u32[]{:S(2)}) collective-permute-start(s32[64,1,128]{2,1,0:T(1,128)} %get-tuple-element.15.m_ref.refs_4_), channel_id=1, source_target_pairs={{0,2},{1,3},{2,0},{3,1},{4,6},{5,7},{6,4},{7,5},{8,10},{9,11},{10,... | collective-permute-start | bytes 98312 | tf_op jit(solution)/shard_map/ppermute | solution.py:606
  51.6 50.7 %collective-permute-start.2 = (s32[64,1,128]{2,1,0:T(1,128)}, s32[64,1,128]{2,1,0:T(1,128)S(1)}, u32[]{:S(2)}, u32[]{:S(2)}) collective-permute-start(s32[64,1,128]{2,1,0:T(1,128)} %get-tuple-element.15.m_ref.refs_4_), channel_id=1, source_target_pairs={{0,3},{1,0},{2,1},{3,2},{4,7},{5,4},{6,5},{7,6},{8,11},{9,8},{10,9... | collective-permute-start | bytes 98312 | tf_op jit(solution)/shard_map/ppermute | solution.py:606
  52.7 51.6 %collective-permute-start = (s32[64,1,128]{2,1,0:T(1,128)}, s32[64,1,128]{2,1,0:T(1,128)S(1)}, u32[]{:S(2)}, u32[]{:S(2)}) collective-permute-start(s32[64,1,128]{2,1,0:T(1,128)} %get-tuple-element.15.m_ref.refs_4_), channel_id=1, source_target_pairs={{0,1},{1,2},{2,3},{3,0},{4,5},{5,6},{6,7},{7,4},{8,9},{9,10},{10,1... | collective-permute-start | bytes 98312 | tf_op jit(solution)/shard_map/ppermute | solution.py:606
  73.5 25.9 %copy-start = (bf16[64,64,128]{2,1,0:T(8,128)(2,1)}, bf16[64,64,128]{2,1,0:T(8,128)(2,1)S(1)}, u32[]{:S(2)}) copy-start(bf16[64,64,128]{2,1,0:T(8,128)(2,1)S(1)} %collective-permute-done.3.refs_9_) | copy-start | bytes 3145732
  73.5 32.6 %collective-permute-start.6 = (bf16[32,64,128]{2,1,0:T(8,128)(2,1)S(1)}, bf16[32,64,128]{2,1,0:T(8,128)(2,1)}, u32[]{:S(2)}, u32[]{:S(2)}) collective-permute-start(bf16[32,64,128]{2,1,0:T(8,128)(2,1)S(1)} %slice.30), channel_id=1, source_target_pairs={{0,3},{1,0},{2,1},{3,2},{4,7},{5,4},{6,5},{7,6},{8,11},{9,8},{10,9... | collective-permute-start | bytes 1572872 | tf_op jit(solution)/shard_map/ppermute | solution.py:606
  77.2 22.2 %copy-start.1 = (bf16[64,64,128]{2,1,0:T(8,128)(2,1)}, bf16[64,64,128]{2,1,0:T(8,128)(2,1)S(1)}, u32[]{:S(2)}) copy-start(bf16[64,64,128]{2,1,0:T(8,128)(2,1)S(1)} %collective-permute-done.1.refs_6_) | copy-start | bytes 3145732
  77.2 28.9 %collective-permute-start.5 = (bf16[32,64,128]{2,1,0:T(8,128)(2,1)S(1)}, bf16[32,64,128]{2,1,0:T(8,128)(2,1)}, u32[]{:S(2)}, u32[]{:S(2)}) collective-permute-start(bf16[32,64,128]{2,1,0:T(8,128)(2,1)S(1)} %slice.29), channel_id=1, source_target_pairs={{0,1},{1,2},{2,3},{3,0},{4,5},{5,6},{6,7},{7,4},{8,9},{9,10},{10,1... | collective-permute-start | bytes 1572872 | tf_op jit(solution)/shard_map/ppermute | solution.py:606
  100.5 5.6 %copy-start.2 = (s32[64,1,128]{2,1,0:T(1,128)}, s32[64,1,128]{2,1,0:T(1,128)S(1)}, u32[]{:S(2)}) copy-start(s32[64,1,128]{2,1,0:T(1,128)S(1)} %collective-permute-done.4.refs_13_.refs_16_) | copy-start | bytes 98308
  102.3 3.8 %copy-start.3 = (s32[64,1,128]{2,1,0:T(1,128)}, s32[64,1,128]{2,1,0:T(1,128)S(1)}, u32[]{:S(2)}) copy-start(s32[64,1,128]{2,1,0:T(1,128)S(1)} %collective-permute-done.2.refs_10_) | copy-start | bytes 98308
  104.2 1.9 copy-start.4

commit v3 on v2

--- a/solution.py
+++ b/solution.py
@@ -15,7 +15,7 @@
 EPSILON = 1e-06
 RIDGE_WEIGHT = 1.0
 NEWTON_STEPS = 8
-UNROLL = 4
+UNROLL = 8
 
 F32 = jnp.float32
 BF16 = jnp.bfloat16
@@ -64,7 +64,7 @@
     lane = lax.broadcasted_iota(I32, (1, 128), 1)
 
     def step(p, carry):
-        block = ids_ref[p]
+        block = ids_ref[p // slots, lax.rem(p, slots)]
         owner = block // BLK_OWN
         tile = p // slots
         code = lax.rem(block, BLK_OWN) * lab_ref.shape[0] + tile
@@ -166,16 +166,16 @@
 
     def step(i, carry):
         spots, sums = [], []
-        for u in range(2):
-            a = 2 * i + u
+        for u in range(4):
+            a = 4 * i + u
             hot = jnp.where(cluster == m_ref[a][:, :rows], 1.0, 0.0).astype(BF16)
             sums.append(jnp.dot(hot, x_ref[a], preferred_element_type=F32))
-            spots.append(code_ref[a] // tiles)
+            spots.append(code_ref[a, 0, rows] // tiles)
         for spot, part in zip(spots, sums):
             sums_ref[spot] += part
         return carry
 
-    lax.fori_loop(0, n // 2, step, 0)
+    lax.fori_loop(0, n // 4, step, 0)
 
     def square(c, total):
         s = sums_ref[c]
@@ -339,8 +339,7 @@
         left = jnp.dot(d, inv, precision=HI, preferred_element_type=F32)
         inv = 2.0 * inv - jnp.dot(inv, left, precision=HI, preferred_element_type=F32)
         low = 4.0 * low / ((1.0 + low) * (1.0 + low))
-    left = jnp.dot(d, inv, precision=HI, preferred_element_type=F32)
-    return 2.0 * inv - jnp.dot(inv, left, precision=HI, preferred_element_type=F32)
+    return inv
 
 
 def scores_kernel(tiles, parts, width, *refs):
@@ -359,14 +358,15 @@
                 a = start + UNROLL * i + u
                 hot = jnp.where(cluster == m_ref[a][:, :rows], 1.0, 0.0).astype(BF16)
                 sums.append(jnp.dot(hot, x_ref[UNROLL * i + u], preferred_element_type=F32))
-                spots.append(code_ref[a] // tiles + base)
+                spots.append(code_ref[a, 0, rows] // tiles + base)
             for spot, part in zip(spots, sums):
                 sums_ref[spot] += part
             return carry
 
         lax.fori_loop(0, count // UNROLL, add, 0)
 
-    scale = jnp.broadcast_to(scale_ref[...], (128, width)).T
+    mine = scale_ref[:, pl.ds(pl.multiple_of(first_ref[0], width), width)]
+    scale = jnp.broadcast_to(mine, (128, width)).T
 
     def normalise(b, carry):
         con_ref[b] = (sums_ref[b] * scale).astype(BF16)
@@ -379,7 +379,7 @@
             spots, values = [], []
             for u in range(UNROLL):
                 a = start + UNROLL * i + u
-                code = code_ref[a]
+                code = code_ref[a, 0, rows]
                 values.append(dot_t(x_ref[UNROLL * i + u], con_ref[code // tiles + base]))
                 spots.append((a, lax.rem(code, tiles)))
             for (a, tile), value in zip(spots, values):
@@ -389,10 +389,9 @@
         lax.fori_loop(0, count // UNROLL, score, 0)
 
 
-def partial_scores(tiles, first, scale, parts, arrays):
+def partial_scores(tiles, width, first, scale, parts, arrays):
     n = arrays[0][2].shape[0]
     rows = arrays[0][1].shape[1]
-    width = scale.shape[1]
     ny = K // width
     flat = [a for group in arrays for a in group]
     return pl.pallas_call(
@@ -442,7 +441,7 @@
 
 
 def reduce_kernel(ny, s_ref, sums_ref, scale_ref, scores_ref, a_ref,
-                  rc, acc, rx, rz, lsem,
+                  rc, acc, rx, rn, rf, lsem,
                   part, gc, a1, gy, a2, gx, a3, gz, gram,
                   cs, cr, xs, xr, zs, zr, ys, yr,
                   gcs, gcr, gys, gyr, gxs, gxr, gzs, gzr,
@@ -489,6 +488,31 @@
         got = lax.rem(x + (s + 2 if down else 2 * NX - s - 2), NX)
         part_z = pl.ds(cut if down else 0, cut)
         acc[got, part_z] += rx[s, part_z]
+
+    docs = rc.shape[2]
+
+    def ahead(side, reach):
+        return lax.rem(z + (NZ - reach if side else reach), NZ)
+
+    def part_d(side):
+        return pl.ds(side * (docs // 2), docs // 2)
+
+    def zcopy(source, target, sem, p):
+        return pltpu.make_async_remote_copy(
+            src_ref=source, dst_ref=target, send_sem=zs.at[sem], recv_sem=zr.at[sem],
+            device_id=dev(x, p, core, y), device_id_type=MESH,
+        )
+
+    def far(side):
+        return zcopy(acc.at[x, ahead(side, 3)], rf.at[side], side, ahead(side, 1))
+
+    def fourth(side):
+        return zcopy(acc.at[x, ahead(side, 4), part_d(side)], rf.at[2, part_d(side)],
+                     2 + side, ahead(side, 2))
+
+    def near(side, reach):
+        slot = 2 * reach - 2 + side
+        return zcopy(acc.at[x, ahead(side, reach)], rn.at[slot], 4 + slot, ahead(side, reach))
 
     blocks = part.shape[0]
     half = blocks // NC
@@ -536,30 +560,48 @@
         land(1, down)
         hop(2, down).start()
     finish()
-    spread(y, ny, peers["y"], lambda p: gram.at[pl.ds(base, quarter)],
-           lambda p: gram.at[pl.ds(core * half + p * quarter, quarter)], gys2, gyr2)()
+    finish = spread(y, ny, peers["y"], lambda p: gram.at[pl.ds(base, quarter)],
+                    lambda p: gram.at[pl.ds(core * half + p * quarter, quarter)], gys2, gyr2)
+    for down in range(2):
+        land(2, down)
+    for side in range(2):
+        far(side).start()
+        fourth(side).start()
+    for side in range(2):
+        near(side, 1).start()
+    finish()
     spread(core, NC, peers["c"], lambda p: gram.at[pl.ds(core * half, half)],
            lambda p: gram.at[pl.ds(p * half, half)], gcs2, gcr2)()
 
     eye = (lax.broadcasted_iota(I32, (K, K), 0) == lax.broadcasted_iota(I32, (K, K), 1)).astype(F32)
     a_ref[...] = gram[...].reshape(K, K) + RIDGE_WEIGHT * eye
-    for down in range(2):
-        land(2, down)
-    finish = spread(z, NZ, peers["z"], lambda p: acc.at[x, p], lambda p: rz.at[p], zs, zr)
-    for p in range(K // 128):
-        inverse_panel(a_ref, p)
-    rz[z] = acc[x, z]
-    finish()
-    total = rz[0]
-    for i in range(1, NZ):
-        total = total + rz[i]
+    inverse_panel(a_ref, 0)
+    for side in range(2):
+        far(side).wait_recv()
+        fourth(side).wait_recv()
+        p = ahead(side, 2)
+        acc[x, p] += rf[side]
+        acc[x, p, part_d(side)] += rf[2, part_d(side)]
+        near(side, 2).start()
+    inverse_panel(a_ref, 1)
+    inverse_panel(a_ref, 2)
+    total = acc[x, z]
+    for side in range(2):
+        for reach in range(1, 3):
+            near(side, reach).wait_recv()
+            total = total + rn[2 * reach - 2 + side]
 
     def lanes(p):
         return pl.ds(pl.multiple_of(p * width, width), width)
 
     scores_ref[:, lanes(y)] = total
-    spread(y, ny, peers["y"], lambda p: scores_ref.at[:, lanes(y)],
-           lambda p: scores_ref.at[:, lanes(p)], ys, yr)()
+    finish = spread(y, ny, peers["y"], lambda p: scores_ref.at[:, lanes(y)],
+                    lambda p: scores_ref.at[:, lanes(p)], ys, yr)
+    inverse_panel(a_ref, 3)
+    finish()
+    for side in range(2):
+        for copy in (far(side), fourth(side), near(side, 1), near(side, 2)):
+            copy.wait_send()
     for copy in swap:
         copy.wait_send()
     for s in range(NX - 1):
@@ -585,7 +627,8 @@
             pltpu.VMEM((NX, NZ, docs, width), F32),
             pltpu.VMEM((NX, NZ, docs, width), F32),
             pltpu.VMEM((NX - 1, NZ, docs, width), F32),
-            pltpu.VMEM((NZ, docs, width), F32),
+            pltpu.VMEM((4, docs, width), F32),
+            pltpu.VMEM((3, docs, width), F32),
             DMA((NX,)),
             pltpu.VMEM((blocks, part_rows, K), F32),
             pltpu.VMEM((half, part_rows, K), F32),
@@ -616,35 +659,31 @@
         assignment.reshape(tiles, 1, rows), ((0, 0), (0, 0), (0, 128 - rows)), constant_values=-1
     )
     ordered, meta = order_blocks(
-        values.reshape(pairs, rows, block_width), block_ids.reshape(pairs), labels
+        values.reshape(pairs, rows, block_width), block_ids, labels
     )
     own_x, own_m = exchange(ordered, meta)
 
-    def code_of(m):
-        return m[:, 0, rows]
-
     half = pairs // 2
-    arrays, parts = [(code_of(own_m), own_x, own_m)], [(0, pairs, 0)]
+    arrays, parts = [(own_m, own_x, own_m)], [(0, pairs, 0)]
     up_x, down_x = shift(own_x, ny, 1), shift(own_x, ny, -1)
     up_m = shift(own_m, ny, 1)
-    arrays.append((code_of(up_m), up_x, up_m))
+    arrays.append((up_m, up_x, up_m))
     parts.append((0, pairs, BLK_OWN))
     if ny > 2:
         down_m, far_m = shift(own_m, ny, -1), shift(own_m, ny, 2)
         far_a = shift(up_x[:half], ny, 1)
         far_b = shift(down_x[half:], ny, -1)
-        arrays.append((code_of(down_m), down_x, down_m))
+        arrays.append((down_m, down_x, down_m))
         parts.append((0, pairs, 3 * BLK_OWN))
-        arrays.append((code_of(far_m), far_a, far_m))
+        arrays.append((far_m, far_a, far_m))
         parts.append((0, half, 2 * BLK_OWN))
-        arrays.append((code_of(far_m), far_b, far_m))
+        arrays.append((far_m, far_b, far_m))
         parts.append((half, half, 2 * BLK_OWN))
 
-    sums, sq = own_sums(tiles, code_of(own_m), own_x, own_m)
+    sums, sq = own_sums(tiles, own_m, own_x, own_m)
     scale = norm_scale(ny, sq)
     first = (y * width).reshape(1)
-    scale_here = lax.dynamic_slice_in_dim(scale, y * width, width, 1)
-    partial = partial_scores(tiles, first, scale_here, tuple(parts), arrays)
+    partial = partial_scores(tiles, width, first, scale, tuple(parts), arrays)
     scores, inverse = reduce_scores(ny, partial, sums, scale)
     inverse_cols = lax.dynamic_slice_in_dim(inverse, y * width, width, 1)
     return jnp.dot(scores, inverse_cols, precision=HI, preferred_element_type=F32)

time: 225 us -> 202 us (0.90)
  Pallas kernels: 192 us -> 176 us
  local copies, waits for them, and re-layouts: 11.9 us -> 1.85 us
  waiting for transfers between devices: 3.19 us -> 8.37 us
    slice x4 -> x0, local copies, waits for them, and re-layouts: 8.25 us -> none  [code_of(): return m[:, 0, rows]]
    pallas_call x1, Pallas kernels: 31.8 us -> 24.8 us  [partial_scores(): pl.pallas_call(functools.partial(scores_kernel, tiles, parts, width), out...]
    ppermute x7, waiting for transfers between devices: 3.19 us -> 8.37 us  [shift(): return lax.ppermute(array, 'terms', [(i, (i + by) % ny) for i in range(ny)])]
    pallas_call x1, Pallas kernels: 82 us -> 78.6 us  [reduce_scores(): pl.pallas_call(functools.partial(reduce_kernel, ny), out_shape=(jax.Shape...]
    pallas_call x1, Pallas kernels: 21.9 us -> 18.9 us  [norm_scale(): pl.pallas_call(functools.partial(norm_kernel, ny), out_shape=jax.ShapeDty...]
    pallas_call x1, Pallas kernels: 14 us -> 11.4 us  [own_sums(): pl.pallas_call(functools.partial(sums_kernel, tiles), out_shape=(jax.Shap...]
  transfers between devices with their start and end apart: 7 -> 7, of which waited for: 1 -> 1; matrix products, arithmetic and copies ran while one was open for 4% -> 0% of each run, Pallas kernels for 16% -> 15%
where the time goes in v3:
time: 202 us; the launch traced here: 201 us
  Pallas kernels  176 us (87%)
  starting transfers between devices  10.7 us (5%)
  waiting for transfers between devices  8.37 us (4%)
  matrix products  2.36 us (1%)
    pallas_call x1, Pallas kernels, reduce_scores(): pl.pallas_call(functools.partial(reduce_kernel, ny), out_shape=(jax.Shape...  78.6 us
    pallas_call x1, Pallas kernels, exchange(): pl.pallas_call(exchange_kernel, out_shape=(jax.ShapeDtypeStruct(x.shape,...  39.2 us
    pallas_call x1, Pallas kernels, partial_scores(): pl.pallas_call(functools.partial(scores_kernel, tiles, parts, width), out...  24.8 us
    pallas_call x1, Pallas kernels, norm_scale(): pl.pallas_call(functools.partial(norm_kernel, ny), out_shape=jax.ShapeDty...  18.9 us
    pallas_call x1, Pallas kernels, own_sums(): pl.pallas_call(functools.partial(sums_kernel, tiles), out_shape=(jax.Shap...  11.4 us
    ppermute x7, starting transfers between devices, shift(): return lax.ppermute(array, 'terms', [(i, (i + by) % ny) for i in range(ny)])  10.7 us
    ppermute x7, waiting for transfers between devices, shift(): return lax.ppermute(array, 'terms', [(i, (i + by) % ny) for i in range(ny)])  8.37 us
  transfers between devices with their start and end apart: 7, of which 1 were waited for; matrix products, arithmetic and copies ran while one was open for 0% of the time, Pallas kernels for 15%

profile of v3, /device:TPU:2, one launch (start us, length us, event | category | flops | bytes accessed | tf_op | source)
XLA Modules:
  0.0 201.2 jit_solution(12119531662201345862)
XLA Ops:
  0.0 0.5 broadcast.5
  0.5 1.3 reduce.3
  1.9 0.1 reshape.14
  1.9 0.6 pad.4.lab_ref
  2.5 3.5 %order_blocks.1 = (bf16[64,64,128]{2,1,0:T(8,128)(2,1)}, s32[64,1,128]{2,1,0:T(1,128)}) custom-call(s32[4,16]{1,0:T(4,128)} %ids_ref.1, bf16[64,64,128]{2,1,0:T(8,128)(2,1)} %bitcast.6, s32[4,1,128]{2,1,0:T(1,128)} %pad.4.lab_ref), custom_call_target="tpu_custom_call" | custom-call | tf_op jit(solution)/shard_map/order_blocks/pallas_call | solution.py:84
  6.0 39.2 %exchange_blocks.1 = (bf16[64,64,128]{2,1,0:T(8,128)(2,1)}, s32[64,1,128]{2,1,0:T(1,128)}) custom-call(bf16[64,64,128]{2,1,0:T(8,128)(2,1)} %get-tuple-element.13.x_ref, s32[64,1,128]{2,1,0:T(1,128)} %get-tuple-element.14.m_ref), custom_call_target="tpu_custom_call" | custom-call | tf_op jit(solution)/shard_map/exchange_blocks/pallas_call | solution.py:151
  45.2 1.7 collective-permute-start.1
  46.9 1.7 collective-permute-start.3
  48.5 0.4 collective-permute-start
  48.9 2.9 %collective-permute-start.2 = (s32[64,1,128]{2,1,0:T(1,128)}, s32[64,1,128]{2,1,0:T(1,128)S(1)}, u32[]{:S(2)}, u32[]{:S(2)}) collective-permute-start(s32[64,1,128]{2,1,0:T(1,128)} %get-tuple-element.15.code_ref.m_ref.refs_2_.refs_4_), channel_id=1, source_target_pairs={{0,3},{1,0},{2,1},{3,2},{4,7},{5,4},{6,5},{7,6},{8,11},{9,8},{10,9... | collective-permute-start | bytes 98312 | tf_op jit(solution)/shard_map/ppermute | solution.py:649
  51.8 0.8 collective-permute-start.4
  52.5 11.4 %own_sums.1 = (f32[32,512,128]{2,1,0:T(8,128)}, f32[1,512]{1,0:T(1,128)}) custom-call(s32[64,1,128]{2,1,0:T(1,128)} %get-tuple-element.15.code_ref.m_ref.refs_2_.refs_4_, bf16[64,64,128]{2,1,0:T(8,128)(2,1)} %get-tuple-element.16.x_ref.refs_3_, s32[64,1,128]{2,1,0:T(1,128)} %get-tuple-element.15.code_ref.m_ref.refs_2_.refs_4_), custom_call_target="tpu_custom_call" | custom-call | flops 8499999744 | bytes 34000000 | tf_op jit(solution)/shard_map/own_sums/pallas_call | solution.py:189
  63.9 8.4 %collective-permute-done.1.refs_6_ = bf16[64,64,128]{2,1,0:T(8,128)(2,1)S(1)} collective-permute-done((bf16[64,64,128]{2,1,0:T(8,128)(2,1)}, bf16[64,64,128]{2,1,0:T(8,128)(2,1)S(1)}, u32[]{:S(2)}, u32[]{:S(2)}) %collective-permute-start.1) | collective-permute-done | bytes 1048608 | tf_op jit(solution)/shard_map/ppermute | solution.py:649
  72.3 0.0 copy-start
  72.3 0.7 collective-permute-start.5
  73.1 0.0 collective-permute-done.3.refs_9_
  73.1 0.0 copy-start.1
  73.1 2.7 %collective-permute-start.6 = (bf16[32,64,128]{2,1,0:T(8,128)(2,1)S(1)}, bf16[32,64,128]{2,1,0:T(8,128)(2,1)}, u32[]{:S(2)}, u32[]{:S(2)}) collective-permute-start(bf16[32,64,128]{2,1,0:T(8,128)(2,1)S(1)} %slice.9), channel_id=1, source_target_pairs={{0,3},{1,0},{2,1},{3,2},{4,7},{5,4},{6,5},{7,6},{8,11},{9,8},{10,9... | collective-permute-start | bytes 1572872 | tf_op jit(solution)/shard_map/ppermute | solution.py:649
  75.8 18.9 %norm_scale.1.refs_1_.scale_ref = f32[1,512]{1,0:T(1,128)} custom-call(f32[1,512]{1,0:T(1,128)} %get-tuple-element.17.sq_ref), custom_call_target="tpu_custom_call" | custom-call | flops 8499999744 | bytes 34000000 | tf_op jit(solution)/shard_map/norm_scale/pallas_call | solution.py:270
  94.7 0.0 copy-done
  94.7 0.0 copy-done.1
  94.7 0.0 collective-permute-done.refs_5_.refs_7_
  94.7 0.0 copy-start.2
  94.7 0.0 collective-permute-done.2.refs_8_.refs_10_
  94.7 0.0 copy-start.3
  94.7 0.0 collective-permute-done.4.refs_11_.refs_13_.refs_14_.refs_16_
  94.8 0.0 copy-start.4
  94.8 0.0 collective-permute-done.5.refs_12_
  94.8 0.0 collective-permute-done.6.refs_15_
  94.8 0.5 copy-done.2
  95.3 0.0 copy-done.3
  95.3 0.0 copy-done.4
  95.4 24.8 %partial_scores.1 = f32[64,4,64,128]{3,2,1,0:T(8,128)} custom-call(s32[1]{0:T(128)} %bitcast.refs_0_, f32[1,512]{1,0:T(1,128)} %norm_scale.1.refs_1_.scale_ref, s32[64,1,128]{2,1,0:T(1,128)} %get-tuple-element.15.code_ref.m_ref.refs_2_.refs_4_, bf16[64,64,128]{2,1,0:T(8,128)(2,1)} %get-tuple-element.16.x_ref.refs_3_, ...), custom_call_target="tpu_custom_call" | custom-call | flops 22499999744 | bytes 90000000 | tf_op jit(solution)/shard_map/partial_scores/pallas_call | solution.py:397
  120.2 78.6 %reduce_scores.1 = (f32[256,512]{1,0:T(8,128)}, f32[512,512]{1,0:T(8,128)}) custom-call(f32[4,8,2,256,128]{4,3,2,1,0:T(8,128)} %bitcast.5, f32[32,512,128]{2,1,0:T(8,128)} %get-tuple-element.18.sums_ref, f32[1,512]{1,0:T(1,128)} %norm_scale.1.refs_1_.scale_ref), custom_call_target="tpu_custom_call" | custom-call | tf_op jit(solution)/shard_map/reduce_scores/pallas_call | solution.py:621
  198.8 2.4 %fusion = f32[256,128]{1,0:T(8,128)} fusion(f32[256,512]{1,0:T(8,128)} %get-tuple-element.19, f32[512,512]{1,0:T(8,128)} %get-tuple-element.20, s32[]{:T(128)S(6)} %select_n.3), kind=kOutput, calls=%fused_computation | convolution fusion | flops 201326592 | bytes 917508 | tf_op jit(solution)/shard_map/dot_general | solution.py:689
  (2 shorter events, 0.1 us)
Async XLA Ops:
  45.2 27.1 %collective-permute-start.1 = (bf16[64,64,128]{2,1,0:T(8,128)(2,1)}, bf16[64,64,128]{2,1,0:T(8,128)(2,1)S(1)}, u32[]{:S(2)}, u32[]{:S(2)}) collective-permute-start(bf16[64,64,128]{2,1,0:T(8,128)(2,1)} %get-tuple-element.16.x_ref.refs_3_), channel_id=1, source_target_pairs={{0,1},{1,2},{2,3},{3,0},{4,5},{5,6},{6,7},{7,4},{8,9},{9,10},{10,1... | collective-permute-start | bytes 3145736 | tf_op jit(solution)/shard_map/ppermute | solution.py:649
  46.9 26.2 %collective-permute-start.3 = (bf16[64,64,128]{2,1,0:T(8,128)(2,1)}, bf16[64,64,128]{2,1,0:T(8,128)(2,1)S(1)}, u32[]{:S(2)}, u32[]{:S(2)}) collective-permute-start(bf16[64,64,128]{2,1,0:T(8,128)(2,1)} %get-tuple-element.16.x_ref.refs_3_), channel_id=1, source_target_pairs={{0,3},{1,0},{2,1},{3,2},{4,7},{5,4},{6,5},{7,6},{8,11},{9,8},{10,9... | collective-permute-start | bytes 3145736 | tf_op jit(solution)/shard_map/ppermute | solution.py:649
  48.5 46.2 %collective-permute-start = (s32[64,1,128]{2,1,0:T(1,128)}, s32[64,1,128]{2,1,0:T(1,128)S(1)}, u32[]{:S(2)}, u32[]{:S(2)}) collective-permute-start(s32[64,1,128]{2,1,0:T(1,128)} %get-tuple-element.15.code_ref.m_ref.refs_2_.refs_4_), channel_id=1, source_target_pairs={{0,1},{1,2},{2,3},{3,0},{4,5},{5,6},{6,7},{7,4},{8,9},{9,10},{10,1... | collective-permute-start | bytes 98312 | tf_op jit(solution)/shard_map/ppermute | solution.py:649
  48.9 45.9 %collective-permute-start.2 = (s32[64,1,128]{2,1,0:T(1,128)}, s32[64,1,128]{2,1,0:T(1,128)S(1)}, u32[]{:S(2)}, u32[]{:S(2)}) collective-permute-start(s32[64,1,128]{2,1,0:T(1,128)} %get-tuple-element.15.code_ref.m_ref.refs_2_.refs_4_), channel_id=1, source_target_pairs={{0,3},{1,0},{2,1},{3,2},{4,7},{5,4},{6,5},{7,6},{8,11},{9,8},{10,9... | collective-permute-start | bytes 98312 | tf_op jit(solution)/shard_map/ppermute | solution.py:649
  51.8 43.0 %collective-permute-start.4 = (s32[64,1,128]{2,1,0:T(1,128)}, s32[64,1,128]{2,1,0:T(1,128)S(1)}, u32[]{:S(2)}, u32[]{:S(2)}) collective-permute-start(s32[64,1,128]{2,1,0:T(1,128)} %get-tuple-element.15.code_ref.m_ref.refs_2_.refs_4_), channel_id=1, source_target_pairs={{0,2},{1,3},{2,0},{3,1},{4,6},{5,7},{6,4},{7,5},{8,10},{9,11},{10,... | collective-permute-start | bytes 98312 | tf_op jit(solution)/shard_map/ppermute | solution.py:649
  72.3 22.4 %copy-start = (bf16[64,64,128]{2,1,0:T(8,128)(2,1)}, bf16[64,64,128]{2,1,0:T(8,128)(2,1)S(1)}, u32[]{:S(2)}) copy-start(bf16[64,64,128]{2,1,0:T(8,128)(2,1)S(1)} %collective-permute-done.1.refs_6_) | copy-start | bytes 3145732
  72.3 22.4 %collective-permute-start.5 = (bf16[32,64,128]{2,1,0:T(8,128)(2,1)S(1)}, bf16[32,64,128]{2,1,0:T(8,128)(2,1)}, u32[]{:S(2)}, u32[]{:S(2)}) collective-permute-start(bf16[32,64,128]{2,1,0:T(8,128)(2,1)S(1)} %slice.8), channel_id=1, source_target_pairs={{0,1},{1,2},{2,3},{3,0},{4,5},{5,6},{6,7},{7,4},{8,9},{9,10},{10,1... | collective-permute-start | bytes 1572872 | tf_op jit(solution)/shard_map/ppermute | solution.py:649
  73.1 21.6 %copy-start.1 = (bf16[64,64,128]{2,1,0:T(8,128)(2,1)}, bf16[64,64,128]{2,1,0:T(8,128)(2,1)S(1)}, u32[]{:S(2)}) copy-start(bf16[64,64,128]{2,1,0:T(8,128)(2,1)S(1)} %collective-permute-done.3.refs_9_) | copy-start | bytes 3145732
  73.1 21.7 %collective-permute-start.6 = (bf16[32,64,128]{2,1,0:T(8,128)(2,1)S(1)}, bf16[32,64,128]{2,1,0:T(8,128)(2,1)}, u32[]{:S(2)}, u32[]{:S(2)}) collective-permute-start(bf16[32,64,128]{2,1,0:T(8,128)(2,1)S(1)} %slice.9), channel_id=1, source_target_pairs={{0,3},{1,0},{2,1},{3,2},{4,7},{5,4},{6,5},{7,6},{8,11},{9,8},{10,9... | collective-permute-start | bytes 1572872 | tf_op jit(solution)/shard_map/ppermute | solution.py:649
  94.7 0.6 copy-start.2
  94.7 0.6 copy-start.3
  94.8 0.6 copy-start.4

commit v4 on v3

--- a/solution.py
+++ b/solution.py
@@ -440,8 +440,8 @@
     a_ref[cut, cut] = inv
 
 
-def reduce_kernel(ny, s_ref, sums_ref, scale_ref, scores_ref, a_ref,
-                  rc, acc, rx, rn, rf, lsem,
+def reduce_kernel(ny, s_ref, sums_hbm, scale_ref, scores_ref, a_ref,
+                  rc, acc, rx, rn, rf, lsem, sums_ref,
                   part, gc, a1, gy, a2, gx, a3, gz, gram,
                   cs, cr, xs, xr, zs, zr, ys, yr,
                   gcs, gcr, gys, gyr, gxs, gxr, gzs, gzr,
@@ -450,6 +450,8 @@
     barrier, count = greet_axes(peers)
     width = rc.shape[-1]
     order = [lax.rem(x + i, NX) for i in (NX - 1, 1, 2, 0)]
+    load = pltpu.make_async_copy(sums_hbm, sums_ref, lsem.at[NX])
+    load.start()
     own = []
     for i, p in enumerate(order):
         copy = pltpu.make_async_copy(s_ref.at[p, :, core], acc.at[p], lsem.at[i])
@@ -474,20 +476,26 @@
     cut = NZ // 2
     upper, lower = peers["x"][0], peers["x"][NX - 2]
 
-    def hop(s, down):
+    def hop(s, down, sub):
         sent = lax.rem(x + (s + 1 if down else 2 * NX - s - 1), NX)
-        part_z = pl.ds(cut if down else 0, cut)
+        part_z = pl.ds(down * cut + sub * (cut // 2), cut // 2)
+        sem = 4 * s + 2 * down + sub
         return pltpu.make_async_remote_copy(
             src_ref=acc.at[sent, part_z], dst_ref=rx.at[s, part_z],
-            send_sem=xs.at[2 * s + down], recv_sem=xr.at[2 * s + down],
+            send_sem=xs.at[sem], recv_sem=xr.at[sem],
             device_id=lower if down else upper, device_id_type=MESH,
         )
 
-    def land(s, down):
-        hop(s, down).wait_recv()
-        got = lax.rem(x + (s + 2 if down else 2 * NX - s - 2), NX)
-        part_z = pl.ds(cut if down else 0, cut)
-        acc[got, part_z] += rx[s, part_z]
+    def land(s, sub):
+        for down in range(2):
+            hop(s, down, sub).wait_recv()
+            got = lax.rem(x + (s + 2 if down else 2 * NX - s - 2), NX)
+            part_z = pl.ds(down * cut + sub * (cut // 2), cut // 2)
+            acc[got, part_z] += rx[s, part_z]
+
+    def go(s, sub):
+        for down in range(2):
+            hop(s, down, sub).start()
 
     docs = rc.shape[2]
 
@@ -518,13 +526,16 @@
     half = blocks // NC
     quarter = half // ny
 
+    load.wait()
     gram_part(sums_ref, scale_ref, part)
     finish = spread(core, NC, peers["c"],
                     lambda p: part.at[pl.ds(p * half, half)], lambda p: gc, gcs, gcr)
     pair(0)
-    hop(0, 0).start()
+    for sub in range(2):
+        hop(0, 0, sub).start()
     pair(1)
-    hop(0, 1).start()
+    for sub in range(2):
+        hop(0, 1, sub).start()
     finish()
     a1[...] = part[pl.ds(core * half, half)] + gc[...]
     finish = spread(y, ny, peers["y"],
@@ -539,16 +550,17 @@
     a2[...] = total
     finish = spread(x, NX, peers["x"], lambda p: a2.at[p], lambda p: gx.at[p], gxs, gxr)
     gx[x] = a2[x]
-    for down in range(2):
-        land(0, down)
-        hop(1, down).start()
+    land(0, 0)
+    go(1, 0)
     finish()
     total = gx[0]
     for i in range(1, NX):
         total = total + gx[i]
     a3[...] = total
     gz[z] = total
-    spread(z, NZ, peers["z"], lambda p: a3, lambda p: gz.at[p], gzs, gzr)()
+    finish = spread(z, NZ, peers["z"], lambda p: a3, lambda p: gz.at[p], gzs, gzr)
+    land(0, 1)
+    finish()
     total = gz[0]
     for i in range(1, NZ):
         total = total + gz[i]
@@ -556,26 +568,29 @@
     gram[base + x] = total
     finish = spread(x, NX, peers["x"], lambda p: gram.at[base + x],
                     lambda p: gram.at[base + p], gxs2, gxr2)
-    for down in range(2):
-        land(1, down)
-        hop(2, down).start()
+    go(1, 1)
+    land(1, 0)
+    go(2, 0)
     finish()
     finish = spread(y, ny, peers["y"], lambda p: gram.at[pl.ds(base, quarter)],
                     lambda p: gram.at[pl.ds(core * half + p * quarter, quarter)], gys2, gyr2)
-    for down in range(2):
-        land(2, down)
+    finish()
+    spread(core, NC, peers["c"], lambda p: gram.at[pl.ds(core * half, half)],
+           lambda p: gram.at[pl.ds(p * half, half)], gcs2, gcr2)()
+    land(1, 1)
+    go(2, 1)
+
+    eye = (lax.broadcasted_iota(I32, (K, K), 0) == lax.broadcasted_iota(I32, (K, K), 1)).astype(F32)
+    a_ref[...] = gram[...].reshape(K, K) + RIDGE_WEIGHT * eye
+    inverse_panel(a_ref, 0)
+    land(2, 0)
+    land(2, 1)
     for side in range(2):
         far(side).start()
         fourth(side).start()
     for side in range(2):
         near(side, 1).start()
-    finish()
-    spread(core, NC, peers["c"], lambda p: gram.at[pl.ds(core * half, half)],
-           lambda p: gram.at[pl.ds(p * half, half)], gcs2, gcr2)()
-
-    eye = (lax.broadcasted_iota(I32, (K, K), 0) == lax.broadcasted_iota(I32, (K, K), 1)).astype(F32)
-    a_ref[...] = gram[...].reshape(K, K) + RIDGE_WEIGHT * eye
-    inverse_panel(a_ref, 0)
+    inverse_panel(a_ref, 1)
     for side in range(2):
         far(side).wait_recv()
         fourth(side).wait_recv()
@@ -583,7 +598,6 @@
         acc[x, p] += rf[side]
         acc[x, p, part_d(side)] += rf[2, part_d(side)]
         near(side, 2).start()
-    inverse_panel(a_ref, 1)
     inverse_panel(a_ref, 2)
     total = acc[x, z]
     for side in range(2):
@@ -606,7 +620,8 @@
         copy.wait_send()
     for s in range(NX - 1):
         for down in range(2):
-            hop(s, down).wait_send()
+            for sub in range(2):
+                hop(s, down, sub).wait_send()
 
 
 def reduce_scores(ny, partial, sums, scale):
@@ -616,12 +631,12 @@
     blocks = K // part_rows
     half, quarter = blocks // NC, blocks // (NC * ny)
     sems = []
-    for size in (NX, 2 * (NX - 1), NZ, ny, NC, ny, NX, NZ, NX, ny, NC):
+    for size in (NX, 4 * (NX - 1), NZ, ny, NC, ny, NX, NZ, NX, ny, NC):
         sems += [DMA((size,)), DMA((size,))]
     return pl.pallas_call(
         functools.partial(reduce_kernel, ny),
         out_shape=(jax.ShapeDtypeStruct((docs, K), F32), jax.ShapeDtypeStruct((K, K), F32)),
-        in_specs=[ANY, VMEM, VMEM],
+        in_specs=[ANY, ANY, VMEM],
         out_specs=(VMEM, VMEM),
         scratch_shapes=[
             pltpu.VMEM((NX, NZ, docs, width), F32),
@@ -629,7 +644,8 @@
             pltpu.VMEM((NX - 1, NZ, docs, width), F32),
             pltpu.VMEM((4, docs, width), F32),
             pltpu.VMEM((3, docs, width), F32),
-            DMA((NX,)),
+            DMA((NX + 1,)),
+            pltpu.VMEM(sums.shape, F32),
             pltpu.VMEM((blocks, part_rows, K), F32),
             pltpu.VMEM((half, part_rows, K), F32),
             pltpu.VMEM((half, part_rows, K), F32),

time: 202 us -> 204 us (level)
  Pallas kernels: 176 us -> 179 us
    pallas_call x1, Pallas kernels: 78.6 us -> 81.3 us  [reduce_scores(): pl.pallas_call(functools.partial(reduce_kernel, ny), out_shape=(jax.Shape...]
where the time goes in v4:
time: 204 us
  Pallas kernels  179 us (88%)
  starting transfers between devices  10.7 us (5%)
  waiting for transfers between devices  8.37 us (4%)
  matrix products  2.36 us (1%)
    pallas_call x1, Pallas kernels, reduce_scores(): pl.pallas_call(functools.partial(reduce_kernel, ny), out_shape=(jax.Shape...  81.3 us
    pallas_call x1, Pallas kernels, exchange(): pl.pallas_call(exchange_kernel, out_shape=(jax.ShapeDtypeStruct(x.shape,...  39.2 us
    pallas_call x1, Pallas kernels, partial_scores(): pl.pallas_call(functools.partial(scores_kernel, tiles, parts, width), out...  24.8 us
    pallas_call x1, Pallas kernels, norm_scale(): pl.pallas_call(functools.partial(norm_kernel, ny), out_shape=jax.ShapeDty...  18.9 us
    pallas_call x1, Pallas kernels, own_sums(): pl.pallas_call(functools.partial(sums_kernel, tiles), out_shape=(jax.Shap...  11.4 us
    ppermute x7, starting transfers between devices, shift(): return lax.ppermute(array, 'terms', [(i, (i + by) % ny) for i in range(ny)])  10.7 us
    ppermute x7, waiting for transfers between devices, shift(): return lax.ppermute(array, 'terms', [(i, (i + by) % ny) for i in range(ny)])  8.37 us
  transfers between devices with their start and end apart: 7, of which 1 were waited for; matrix products, arithmetic and copies ran while one was open for 0% of the time, Pallas kernels for 15%

profile of v4, /device:TPU:2, one launch (start us, length us, event | category | flops | bytes accessed | tf_op | source)
XLA Modules:
  0.0 203.9 jit_solution(2234539046381689832)
XLA Ops:
  0.0 0.5 broadcast.5
  0.5 1.3 reduce.3
  1.9 0.1 reshape.14
  1.9 0.6 pad.4.lab_ref
  2.5 3.5 %order_blocks.1 = (bf16[64,64,128]{2,1,0:T(8,128)(2,1)}, s32[64,1,128]{2,1,0:T(1,128)}) custom-call(s32[4,16]{1,0:T(4,128)} %ids_ref.1, bf16[64,64,128]{2,1,0:T(8,128)(2,1)} %bitcast.6, s32[4,1,128]{2,1,0:T(1,128)} %pad.4.lab_ref), custom_call_target="tpu_custom_call" | custom-call | tf_op jit(solution)/shard_map/order_blocks/pallas_call | solution.py:84
  6.0 39.2 %exchange_blocks.1 = (bf16[64,64,128]{2,1,0:T(8,128)(2,1)}, s32[64,1,128]{2,1,0:T(1,128)}) custom-call(bf16[64,64,128]{2,1,0:T(8,128)(2,1)} %get-tuple-element.13.x_ref, s32[64,1,128]{2,1,0:T(1,128)} %get-tuple-element.14.m_ref), custom_call_target="tpu_custom_call" | custom-call | tf_op jit(solution)/shard_map/exchange_blocks/pallas_call | solution.py:151
  45.2 1.7 collective-permute-start.1
  46.9 1.7 collective-permute-start.3
  48.5 0.4 collective-permute-start
  48.9 2.9 %collective-permute-start.2 = (s32[64,1,128]{2,1,0:T(1,128)}, s32[64,1,128]{2,1,0:T(1,128)S(1)}, u32[]{:S(2)}, u32[]{:S(2)}) collective-permute-start(s32[64,1,128]{2,1,0:T(1,128)} %get-tuple-element.15.code_ref.m_ref.refs_2_.refs_4_), channel_id=1, source_target_pairs={{0,3},{1,0},{2,1},{3,2},{4,7},{5,4},{6,5},{7,6},{8,11},{9,8},{10,9... | collective-permute-start | bytes 98312 | tf_op jit(solution)/shard_map/ppermute | solution.py:665
  51.8 0.8 collective-permute-start.4
  52.5 11.4 %own_sums.1 = (f32[32,512,128]{2,1,0:T(8,128)}, f32[1,512]{1,0:T(1,128)}) custom-call(s32[64,1,128]{2,1,0:T(1,128)} %get-tuple-element.15.code_ref.m_ref.refs_2_.refs_4_, bf16[64,64,128]{2,1,0:T(8,128)(2,1)} %get-tuple-element.16.x_ref.refs_3_, s32[64,1,128]{2,1,0:T(1,128)} %get-tuple-element.15.code_ref.m_ref.refs_2_.refs_4_), custom_call_target="tpu_custom_call" | custom-call | flops 8499999744 | bytes 34000000 | tf_op jit(solution)/shard_map/own_sums/pallas_call | solution.py:189
  63.9 8.4 %collective-permute-done.1.refs_6_ = bf16[64,64,128]{2,1,0:T(8,128)(2,1)S(1)} collective-permute-done((bf16[64,64,128]{2,1,0:T(8,128)(2,1)}, bf16[64,64,128]{2,1,0:T(8,128)(2,1)S(1)}, u32[]{:S(2)}, u32[]{:S(2)}) %collective-permute-start.1) | collective-permute-done | bytes 1048608 | tf_op jit(solution)/shard_map/ppermute | solution.py:665
  72.3 0.0 copy-start
  72.3 0.7 collective-permute-start.5
  73.1 0.0 collective-permute-done.3.refs_9_
  73.1 0.0 copy-start.1
  73.1 2.7 %collective-permute-start.6 = (bf16[32,64,128]{2,1,0:T(8,128)(2,1)S(1)}, bf16[32,64,128]{2,1,0:T(8,128)(2,1)}, u32[]{:S(2)}, u32[]{:S(2)}) collective-permute-start(bf16[32,64,128]{2,1,0:T(8,128)(2,1)S(1)} %slice.9), channel_id=1, source_target_pairs={{0,3},{1,0},{2,1},{3,2},{4,7},{5,4},{6,5},{7,6},{8,11},{9,8},{10,9... | collective-permute-start | bytes 1572872 | tf_op jit(solution)/shard_map/ppermute | solution.py:665
  75.8 18.9 %norm_scale.1.refs_1_.scale_ref = f32[1,512]{1,0:T(1,128)} custom-call(f32[1,512]{1,0:T(1,128)} %get-tuple-element.17.sq_ref), custom_call_target="tpu_custom_call" | custom-call | flops 8499999744 | bytes 34000000 | tf_op jit(solution)/shard_map/norm_scale/pallas_call | solution.py:270
  94.7 0.0 copy-done
  94.7 0.0 copy-done.1
  94.7 0.0 collective-permute-done.refs_5_.refs_7_
  94.7 0.0 copy-start.2
  94.7 0.0 collective-permute-done.2.refs_8_.refs_10_
  94.7 0.0 copy-start.3
  94.7 0.0 collective-permute-done.4.refs_11_.refs_13_.refs_14_.refs_16_
  94.8 0.0 copy-start.4
  94.8 0.0 collective-permute-done.5.refs_12_
  94.8 0.0 collective-permute-done.6.refs_15_
  94.8 0.5 copy-done.2
  95.3 0.0 copy-done.3
  95.3 0.0 copy-done.4
  95.4 24.8 %partial_scores.1 = f32[64,4,64,128]{3,2,1,0:T(8,128)} custom-call(s32[1]{0:T(128)} %bitcast.refs_0_, f32[1,512]{1,0:T(1,128)} %norm_scale.1.refs_1_.scale_ref, s32[64,1,128]{2,1,0:T(1,128)} %get-tuple-element.15.code_ref.m_ref.refs_2_.refs_4_, bf16[64,64,128]{2,1,0:T(8,128)(2,1)} %get-tuple-element.16.x_ref.refs_3_, ...), custom_call_target="tpu_custom_call" | custom-call | flops 22499999744 | bytes 90000000 | tf_op jit(solution)/shard_map/partial_scores/pallas_call | solution.py:397
  120.2 81.3 %reduce_scores.1 = (f32[256,512]{1,0:T(8,128)}, f32[512,512]{1,0:T(8,128)}) custom-call(f32[4,8,2,256,128]{4,3,2,1,0:T(8,128)} %bitcast.5, f32[32,512,128]{2,1,0:T(8,128)} %get-tuple-element.18.sums_hbm, f32[1,512]{1,0:T(1,128)} %norm_scale.1.refs_1_.scale_ref), custom_call_target="tpu_custom_call" | custom-call | tf_op jit(solution)/shard_map/reduce_scores/pallas_call | solution.py:636
  201.5 2.4 %fusion = f32[256,128]{1,0:T(8,128)} fusion(f32[256,512]{1,0:T(8,128)} %get-tuple-element.19, f32[512,512]{1,0:T(8,128)} %get-tuple-element.20, s32[]{:T(128)S(6)} %select_n.3), kind=kOutput, calls=%fused_computation | convolution fusion | flops 201326592 | bytes 917508 | tf_op jit(solution)/shard_map/dot_general | solution.py:705
  (2 shorter events, 0.1 us)
Async XLA Ops:
  45.2 27.1 %collective-permute-start.1 = (bf16[64,64,128]{2,1,0:T(8,128)(2,1)}, bf16[64,64,128]{2,1,0:T(8,128)(2,1)S(1)}, u32[]{:S(2)}, u32[]{:S(2)}) collective-permute-start(bf16[64,64,128]{2,1,0:T(8,128)(2,1)} %get-tuple-element.16.x_ref.refs_3_), channel_id=1, source_target_pairs={{0,1},{1,2},{2,3},{3,0},{4,5},{5,6},{6,7},{7,4},{8,9},{9,10},{10,1... | collective-permute-start | bytes 3145736 | tf_op jit(solution)/shard_map/ppermute | solution.py:665
  46.9 26.2 %collective-permute-start.3 = (bf16[64,64,128]{2,1,0:T(8,128)(2,1)}, bf16[64,64,128]{2,1,0:T(8,128)(2,1)S(1)}, u32[]{:S(2)}, u32[]{:S(2)}) collective-permute-start(bf16[64,64,128]{2,1,0:T(8,128)(2,1)} %get-tuple-element.16.x_ref.refs_3_), channel_id=1, source_target_pairs={{0,3},{1,0},{2,1},{3,2},{4,7},{5,4},{6,5},{7,6},{8,11},{9,8},{10,9... | collective-permute-start | bytes 3145736 | tf_op jit(solution)/shard_map/ppermute | solution.py:665
  48.5 46.2 %collective-permute-start = (s32[64,1,128]{2,1,0:T(1,128)}, s32[64,1,128]{2,1,0:T(1,128)S(1)}, u32[]{:S(2)}, u32[]{:S(2)}) collective-permute-start(s32[64,1,128]{2,1,0:T(1,128)} %get-tuple-element.15.code_ref.m_ref.refs_2_.refs_4_), channel_id=1, source_target_pairs={{0,1},{1,2},{2,3},{3,0},{4,5},{5,6},{6,7},{7,4},{8,9},{9,10},{10,1... | collective-permute-start | bytes 98312 | tf_op jit(solution)/shard_map/ppermute | solution.py:665
  48.9 45.9 %collective-permute-start.2 = (s32[64,1,128]{2,1,0:T(1,128)}, s32[64,1,128]{2,1,0:T(1,128)S(1)}, u32[]{:S(2)}, u32[]{:S(2)}) collective-permute-start(s32[64,1,128]{2,1,0:T(1,128)} %get-tuple-element.15.code_ref.m_ref.refs_2_.refs_4_), channel_id=1, source_target_pairs={{0,3},{1,0},{2,1},{3,2},{4,7},{5,4},{6,5},{7,6},{8,11},{9,8},{10,9... | collective-permute-start | bytes 98312 | tf_op jit(solution)/shard_map/ppermute | solution.py:665
  51.8 43.0 %collective-permute-start.4 = (s32[64,1,128]{2,1,0:T(1,128)}, s32[64,1,128]{2,1,0:T(1,128)S(1)}, u32[]{:S(2)}, u32[]{:S(2)}) collective-permute-start(s32[64,1,128]{2,1,0:T(1,128)} %get-tuple-element.15.code_ref.m_ref.refs_2_.refs_4_), channel_id=1, source_target_pairs={{0,2},{1,3},{2,0},{3,1},{4,6},{5,7},{6,4},{7,5},{8,10},{9,11},{10,... | collective-permute-start | bytes 98312 | tf_op jit(solution)/shard_map/ppermute | solution.py:665
  72.3 22.4 %copy-start = (bf16[64,64,128]{2,1,0:T(8,128)(2,1)}, bf16[64,64,128]{2,1,0:T(8,128)(2,1)S(1)}, u32[]{:S(2)}) copy-start(bf16[64,64,128]{2,1,0:T(8,128)(2,1)S(1)} %collective-permute-done.1.refs_6_) | copy-start | bytes 3145732
  72.3 22.4 %collective-permute-start.5 = (bf16[32,64,128]{2,1,0:T(8,128)(2,1)S(1)}, bf16[32,64,128]{2,1,0:T(8,128)(2,1)}, u32[]{:S(2)}, u32[]{:S(2)}) collective-permute-start(bf16[32,64,128]{2,1,0:T(8,128)(2,1)S(1)} %slice.8), channel_id=1, source_target_pairs={{0,1},{1,2},{2,3},{3,0},{4,5},{5,6},{6,7},{7,4},{8,9},{9,10},{10,1... | collective-permute-start | bytes 1572872 | tf_op jit(solution)/shard_map/ppermute | solution.py:665
  73.1 21.6 %copy-start.1 = (bf16[64,64,128]{2,1,0:T(8,128)(2,1)}, bf16[64,64,128]{2,1,0:T(8,128)(2,1)S(1)}, u32[]{:S(2)}) copy-start(bf16[64,64,128]{2,1,0:T(8,128)(2,1)S(1)} %collective-permute-done.3.refs_9_) | copy-start | bytes 3145732
  73.1 21.7 %collective-permute-start.6 = (bf16[32,64,128]{2,1,0:T(8,128)(2,1)S(1)}, bf16[32,64,128]{2,1,0:T(8,128)(2,1)}, u32[]{:S(2)}, u32[]{:S(2)}) collective-permute-start(bf16[32,64,128]{2,1,0:T(8,128)(2,1)S(1)} %slice.9), channel_id=1, source_target_pairs={{0,3},{1,0},{2,1},{3,2},{4,7},{5,4},{6,5},{7,6},{8,11},{9,8},{10,9... | collective-permute-start | bytes 1572872 | tf_op jit(solution)/shard_map/ppermute | solution.py:665
  94.7 0.6 copy-start.2
  94.7 0.6 copy-start.3
  94.8 0.6 copy-start.4

commit v5 on v4

--- a/solution.py
+++ b/solution.py
@@ -574,15 +574,14 @@
     finish()
     finish = spread(y, ny, peers["y"], lambda p: gram.at[pl.ds(base, quarter)],
                     lambda p: gram.at[pl.ds(core * half + p * quarter, quarter)], gys2, gyr2)
+    land(1, 1)
+    go(2, 1)
     finish()
     spread(core, NC, peers["c"], lambda p: gram.at[pl.ds(core * half, half)],
            lambda p: gram.at[pl.ds(p * half, half)], gcs2, gcr2)()
-    land(1, 1)
-    go(2, 1)
 
     eye = (lax.broadcasted_iota(I32, (K, K), 0) == lax.broadcasted_iota(I32, (K, K), 1)).astype(F32)
     a_ref[...] = gram[...].reshape(K, K) + RIDGE_WEIGHT * eye
-    inverse_panel(a_ref, 0)
     land(2, 0)
     land(2, 1)
     for side in range(2):
@@ -590,7 +589,7 @@
         fourth(side).start()
     for side in range(2):
         near(side, 1).start()
-    inverse_panel(a_ref, 1)
+    inverse_panel(a_ref, 0)
     for side in range(2):
         far(side).wait_recv()
         fourth(side).wait_recv()
@@ -598,6 +597,7 @@
         acc[x, p] += rf[side]
         acc[x, p, part_d(side)] += rf[2, part_d(side)]
         near(side, 2).start()
+    inverse_panel(a_ref, 1)
     inverse_panel(a_ref, 2)
     total = acc[x, z]
     for side in range(2):

time: 204 us -> 204 us (level)
  no operation moved by 1% of the time
where the time goes in v5:
time: 204 us
  Pallas kernels  179 us (88%)
  starting transfers between devices  10.7 us (5%)
  waiting for transfers between devices  8.37 us (4%)
  matrix products  2.36 us (1%)
    pallas_call x1, Pallas kernels, reduce_scores(): pl.pallas_call(functools.partial(reduce_kernel, ny), out_shape=(jax.Shape...  81.6 us
    pallas_call x1, Pallas kernels, exchange(): pl.pallas_call(exchange_kernel, out_shape=(jax.ShapeDtypeStruct(x.shape,...  39.2 us
    pallas_call x1, Pallas kernels, partial_scores(): pl.pallas_call(functools.partial(scores_kernel, tiles, parts, width), out...  24.8 us
    pallas_call x1, Pallas kernels, norm_scale(): pl.pallas_call(functools.partial(norm_kernel, ny), out_shape=jax.ShapeDty...  18.9 us
    pallas_call x1, Pallas kernels, own_sums(): pl.pallas_call(functools.partial(sums_kernel, tiles), out_shape=(jax.Shap...  11.4 us
    ppermute x7, starting transfers between devices, shift(): return lax.ppermute(array, 'terms', [(i, (i + by) % ny) for i in range(ny)])  10.7 us
    ppermute x7, waiting for transfers between devices, shift(): return lax.ppermute(array, 'terms', [(i, (i + by) % ny) for i in range(ny)])  8.37 us
  transfers between devices with their start and end apart: 7, of which 1 were waited for; matrix products, arithmetic and copies ran while one was open for 0% of the time, Pallas kernels for 15%

profile of v5, /device:TPU:2, one launch (start us, length us, event | category | flops | bytes accessed | tf_op | source)
XLA Modules:
  0.0 204.1 jit_solution(9007551363399677195)
XLA Ops:
  0.0 0.5 broadcast.5
  0.5 1.3 reduce.3
  1.9 0.1 reshape.14
  1.9 0.6 pad.4.lab_ref
  2.5 3.5 %order_blocks.1 = (bf16[64,64,128]{2,1,0:T(8,128)(2,1)}, s32[64,1,128]{2,1,0:T(1,128)}) custom-call(s32[4,16]{1,0:T(4,128)} %ids_ref.1, bf16[64,64,128]{2,1,0:T(8,128)(2,1)} %bitcast.6, s32[4,1,128]{2,1,0:T(1,128)} %pad.4.lab_ref), custom_call_target="tpu_custom_call" | custom-call | tf_op jit(solution)/shard_map/order_blocks/pallas_call | solution.py:84
  6.0 39.2 %exchange_blocks.1 = (bf16[64,64,128]{2,1,0:T(8,128)(2,1)}, s32[64,1,128]{2,1,0:T(1,128)}) custom-call(bf16[64,64,128]{2,1,0:T(8,128)(2,1)} %get-tuple-element.13.x_ref, s32[64,1,128]{2,1,0:T(1,128)} %get-tuple-element.14.m_ref), custom_call_target="tpu_custom_call" | custom-call | tf_op jit(solution)/shard_map/exchange_blocks/pallas_call | solution.py:151
  45.2 1.7 collective-permute-start.1
  46.9 1.7 collective-permute-start.3
  48.5 0.4 collective-permute-start
  48.9 2.9 %collective-permute-start.2 = (s32[64,1,128]{2,1,0:T(1,128)}, s32[64,1,128]{2,1,0:T(1,128)S(1)}, u32[]{:S(2)}, u32[]{:S(2)}) collective-permute-start(s32[64,1,128]{2,1,0:T(1,128)} %get-tuple-element.15.code_ref.m_ref.refs_2_.refs_4_), channel_id=1, source_target_pairs={{0,3},{1,0},{2,1},{3,2},{4,7},{5,4},{6,5},{7,6},{8,11},{9,8},{10,9... | collective-permute-start | bytes 98312 | tf_op jit(solution)/shard_map/ppermute | solution.py:665
  51.8 0.8 collective-permute-start.4
  52.5 11.4 %own_sums.1 = (f32[32,512,128]{2,1,0:T(8,128)}, f32[1,512]{1,0:T(1,128)}) custom-call(s32[64,1,128]{2,1,0:T(1,128)} %get-tuple-element.15.code_ref.m_ref.refs_2_.refs_4_, bf16[64,64,128]{2,1,0:T(8,128)(2,1)} %get-tuple-element.16.x_ref.refs_3_, s32[64,1,128]{2,1,0:T(1,128)} %get-tuple-element.15.code_ref.m_ref.refs_2_.refs_4_), custom_call_target="tpu_custom_call" | custom-call | flops 8499999744 | bytes 34000000 | tf_op jit(solution)/shard_map/own_sums/pallas_call | solution.py:189
  63.9 8.4 %collective-permute-done.1.refs_6_ = bf16[64,64,128]{2,1,0:T(8,128)(2,1)S(1)} collective-permute-done((bf16[64,64,128]{2,1,0:T(8,128)(2,1)}, bf16[64,64,128]{2,1,0:T(8,128)(2,1)S(1)}, u32[]{:S(2)}, u32[]{:S(2)}) %collective-permute-start.1) | collective-permute-done | bytes 1048608 | tf_op jit(solution)/shard_map/ppermute | solution.py:665
  72.3 0.0 copy-start
  72.3 0.7 collective-permute-start.5
  73.1 0.0 collective-permute-done.3.refs_9_
  73.1 0.0 copy-start.1
  73.1 2.7 %collective-permute-start.6 = (bf16[32,64,128]{2,1,0:T(8,128)(2,1)S(1)}, bf16[32,64,128]{2,1,0:T(8,128)(2,1)}, u32[]{:S(2)}, u32[]{:S(2)}) collective-permute-start(bf16[32,64,128]{2,1,0:T(8,128)(2,1)S(1)} %slice.9), channel_id=1, source_target_pairs={{0,3},{1,0},{2,1},{3,2},{4,7},{5,4},{6,5},{7,6},{8,11},{9,8},{10,9... | collective-permute-start | bytes 1572872 | tf_op jit(solution)/shard_map/ppermute | solution.py:665
  75.8 18.9 %norm_scale.1.refs_1_.scale_ref = f32[1,512]{1,0:T(1,128)} custom-call(f32[1,512]{1,0:T(1,128)} %get-tuple-element.17.sq_ref), custom_call_target="tpu_custom_call" | custom-call | flops 8499999744 | bytes 34000000 | tf_op jit(solution)/shard_map/norm_scale/pallas_call | solution.py:270
  94.7 0.0 copy-done
  94.7 0.0 copy-done.1
  94.7 0.0 collective-permute-done.refs_5_.refs_7_
  94.7 0.0 copy-start.2
  94.7 0.0 collective-permute-done.2.refs_8_.refs_10_
  94.7 0.0 copy-start.3
  94.7 0.0 collective-permute-done.4.refs_11_.refs_13_.refs_14_.refs_16_
  94.8 0.0 copy-start.4
  94.8 0.0 collective-permute-done.5.refs_12_
  94.8 0.0 collective-permute-done.6.refs_15_
  94.8 0.5 copy-done.2
  95.3 0.0 copy-done.3
  95.3 0.0 copy-done.4
  95.4 24.8 %partial_scores.1 = f32[64,4,64,128]{3,2,1,0:T(8,128)} custom-call(s32[1]{0:T(128)} %bitcast.refs_0_, f32[1,512]{1,0:T(1,128)} %norm_scale.1.refs_1_.scale_ref, s32[64,1,128]{2,1,0:T(1,128)} %get-tuple-element.15.code_ref.m_ref.refs_2_.refs_4_, bf16[64,64,128]{2,1,0:T(8,128)(2,1)} %get-tuple-element.16.x_ref.refs_3_, ...), custom_call_target="tpu_custom_call" | custom-call | flops 22499999744 | bytes 90000000 | tf_op jit(solution)/shard_map/partial_scores/pallas_call | solution.py:397
  120.2 81.6 %reduce_scores.1 = (f32[256,512]{1,0:T(8,128)}, f32[512,512]{1,0:T(8,128)}) custom-call(f32[4,8,2,256,128]{4,3,2,1,0:T(8,128)} %bitcast.5, f32[32,512,128]{2,1,0:T(8,128)} %get-tuple-element.18.sums_hbm, f32[1,512]{1,0:T(1,128)} %norm_scale.1.refs_1_.scale_ref), custom_call_target="tpu_custom_call" | custom-call | tf_op jit(solution)/shard_map/reduce_scores/pallas_call | solution.py:636
  201.8 2.4 %fusion = f32[256,128]{1,0:T(8,128)} fusion(f32[256,512]{1,0:T(8,128)} %get-tuple-element.19, f32[512,512]{1,0:T(8,128)} %get-tuple-element.20, s32[]{:T(128)S(6)} %select_n.3), kind=kOutput, calls=%fused_computation | convolution fusion | flops 201326592 | bytes 917508 | tf_op jit(solution)/shard_map/dot_general | solution.py:705
  (2 shorter events, 0.1 us)
Async XLA Ops:
  45.2 27.1 %collective-permute-start.1 = (bf16[64,64,128]{2,1,0:T(8,128)(2,1)}, bf16[64,64,128]{2,1,0:T(8,128)(2,1)S(1)}, u32[]{:S(2)}, u32[]{:S(2)}) collective-permute-start(bf16[64,64,128]{2,1,0:T(8,128)(2,1)} %get-tuple-element.16.x_ref.refs_3_), channel_id=1, source_target_pairs={{0,1},{1,2},{2,3},{3,0},{4,5},{5,6},{6,7},{7,4},{8,9},{9,10},{10,1... | collective-permute-start | bytes 3145736 | tf_op jit(solution)/shard_map/ppermute | solution.py:665
  46.9 26.2 %collective-permute-start.3 = (bf16[64,64,128]{2,1,0:T(8,128)(2,1)}, bf16[64,64,128]{2,1,0:T(8,128)(2,1)S(1)}, u32[]{:S(2)}, u32[]{:S(2)}) collective-permute-start(bf16[64,64,128]{2,1,0:T(8,128)(2,1)} %get-tuple-element.16.x_ref.refs_3_), channel_id=1, source_target_pairs={{0,3},{1,0},{2,1},{3,2},{4,7},{5,4},{6,5},{7,6},{8,11},{9,8},{10,9... | collective-permute-start | bytes 3145736 | tf_op jit(solution)/shard_map/ppermute | solution.py:665
  48.5 46.2 %collective-permute-start = (s32[64,1,128]{2,1,0:T(1,128)}, s32[64,1,128]{2,1,0:T(1,128)S(1)}, u32[]{:S(2)}, u32[]{:S(2)}) collective-permute-start(s32[64,1,128]{2,1,0:T(1,128)} %get-tuple-element.15.code_ref.m_ref.refs_2_.refs_4_), channel_id=1, source_target_pairs={{0,1},{1,2},{2,3},{3,0},{4,5},{5,6},{6,7},{7,4},{8,9},{9,10},{10,1... | collective-permute-start | bytes 98312 | tf_op jit(solution)/shard_map/ppermute | solution.py:665
  48.9 45.9 %collective-permute-start.2 = (s32[64,1,128]{2,1,0:T(1,128)}, s32[64,1,128]{2,1,0:T(1,128)S(1)}, u32[]{:S(2)}, u32[]{:S(2)}) collective-permute-start(s32[64,1,128]{2,1,0:T(1,128)} %get-tuple-element.15.code_ref.m_ref.refs_2_.refs_4_), channel_id=1, source_target_pairs={{0,3},{1,0},{2,1},{3,2},{4,7},{5,4},{6,5},{7,6},{8,11},{9,8},{10,9... | collective-permute-start | bytes 98312 | tf_op jit(solution)/shard_map/ppermute | solution.py:665
  51.8 43.0 %collective-permute-start.4 = (s32[64,1,128]{2,1,0:T(1,128)}, s32[64,1,128]{2,1,0:T(1,128)S(1)}, u32[]{:S(2)}, u32[]{:S(2)}) collective-permute-start(s32[64,1,128]{2,1,0:T(1,128)} %get-tuple-element.15.code_ref.m_ref.refs_2_.refs_4_), channel_id=1, source_target_pairs={{0,2},{1,3},{2,0},{3,1},{4,6},{5,7},{6,4},{7,5},{8,10},{9,11},{10,... | collective-permute-start | bytes 98312 | tf_op jit(solution)/shard_map/ppermute | solution.py:665
  72.3 22.4 %copy-start = (bf16[64,64,128]{2,1,0:T(8,128)(2,1)}, bf16[64,64,128]{2,1,0:T(8,128)(2,1)S(1)}, u32[]{:S(2)}) copy-start(bf16[64,64,128]{2,1,0:T(8,128)(2,1)S(1)} %collective-permute-done.1.refs_6_) | copy-start | bytes 3145732
  72.3 22.4 %collective-permute-start.5 = (bf16[32,64,128]{2,1,0:T(8,128)(2,1)S(1)}, bf16[32,64,128]{2,1,0:T(8,128)(2,1)}, u32[]{:S(2)}, u32[]{:S(2)}) collective-permute-start(bf16[32,64,128]{2,1,0:T(8,128)(2,1)S(1)} %slice.8), channel_id=1, source_target_pairs={{0,1},{1,2},{2,3},{3,0},{4,5},{5,6},{6,7},{7,4},{8,9},{9,10},{10,1... | collective-permute-start | bytes 1572872 | tf_op jit(solution)/shard_map/ppermute | solution.py:665
  73.1 21.6 %copy-start.1 = (bf16[64,64,128]{2,1,0:T(8,128)(2,1)}, bf16[64,64,128]{2,1,0:T(8,128)(2,1)S(1)}, u32[]{:S(2)}) copy-start(bf16[64,64,128]{2,1,0:T(8,128)(2,1)S(1)} %collective-permute-done.3.refs_9_) | copy-start | bytes 3145732
  73.1 21.7 %collective-permute-start.6 = (bf16[32,64,128]{2,1,0:T(8,128)(2,1)S(1)}, bf16[32,64,128]{2,1,0:T(8,128)(2,1)}, u32[]{:S(2)}, u32[]{:S(2)}) collective-permute-start(bf16[32,64,128]{2,1,0:T(8,128)(2,1)S(1)} %slice.9), channel_id=1, source_target_pairs={{0,3},{1,0},{2,1},{3,2},{4,7},{5,4},{6,5},{7,6},{8,11},{9,8},{10,9... | collective-permute-start | bytes 1572872 | tf_op jit(solution)/shard_map/ppermute | solution.py:665
  94.7 0.6 copy-start.2
  94.7 0.6 copy-start.3
  94.8 0.6 copy-start.4
